TPU v7x, 128 devices: a whole 4x4x4 slice. The times are simulated.
128 devices in a mesh: role: 2 (over x_hi), shard: 16 (over z, y), rep: 4 (over x_lo, core).
Axes of the slice: x: 4 (x_hi: 2, x_lo: 2; x = x_hi * 2 + x_lo), y: 4, z: 4, core: 2. Of those that a mesh axis runs over, the one named last changes fastest.
Arguments:
- qkv_versions: bfloat16 [2, 5120, 7168], P('role', 'rep', 'shard'), may hold values from -0.078125 to 0.078125
- qkv_bias: bfloat16 [2, 7168], P('role'), may hold values from -3 to 3
- o_versions: bfloat16 [2, 5120, 5120], P('role', 'rep', 'shard'), may hold values from -0.078125 to 0.078125
- norm_gain: bfloat16 [2, 5120], P('role'), may hold values from 0.5 to 1.5
- hidden: bfloat16 [2, 1024, 4, 5120], P('role', ('shard', 'rep')), may hold values from -6 to 6
- cache_keys: bfloat16 [2, 1024, 128, 1024], P('role', ('shard', 'rep')), may hold values from -220 to 220
- cache_values: bfloat16 [2, 1024, 128, 1024], P('role', ('shard', 'rep')), may hold values from -6 to 6
- lengths: int32 [2, 1024], P('role', ('shard', 'rep')), may hold values from 2 to 128, as said below
Outputs:
- layer_out: bfloat16 [2, 1024, 4, 5120], P('role', ('shard', 'rep'))
- new_qkv: bfloat16 [2, 5120, 7168], P('role', 'rep', 'shard')
- new_o: bfloat16 [2, 5120, 5120], P('role', 'rep', 'shard')
Inputs may be any that keep to these rules, and one draw needn't show every extreme that they name: `lengths`: in every aligned group of 16 rows of a role at least one row has all 128 positions live.
All inputs are finite; a program needn't handle non-finite values.
Results may differ from a plain program's by a relative error of at most 0.0065.
The roundings to bfloat16 on the way count: a program that leaves them out, or rounds other values in their place, can miss the bound.
Values may be sent and summed in bfloat16 or wider, within the bound.
No kernel may reach another device: no remote copies, remote signals or barrier semaphores. Data moves between devices by JAX's collectives and lax.ppermute only.
A program may use at most 128 MiB of HBM per device.

v0:
```python
import functools
import math

import jax
import jax.numpy as jnp
from jax import lax
from jax.experimental import pallas as pl
from jax.experimental.pallas import tpu as pltpu
from jax.sharding import PartitionSpec as P


FACTOR_A = 40
FACTOR_B = 128
D = 5120
HEADS = 40
KV_HEADS = 8
HEAD_DIM = 128
QDIM = 5120
KVD = 1024
STEPS = 4


EPSILON = 1e-06
ROPE_BASE = 1000000.0


LINES = 4


def shifted(value, axis, steps):
    count = lax.axis_size(axis)
    initial, last = (max(0, -steps), min(count, count - steps))
    return lax.ppermute(value, axis, [(source, source + steps) for source in range(initial, last)])


def along_z(value, steps):
    count = lax.axis_size("shard")
    pairs = [(s, (s + steps * LINES) % count) for s in range(count)]
    return lax.ppermute(value, "shard", pairs)


def mirror_y(value):
    count = lax.axis_size("shard")
    return lax.ppermute(value, "shard", [(s, s ^ 3) for s in range(count)])


def next_y(value):
    count = lax.axis_size("shard")
    return lax.ppermute(value, "shard", [(s, s ^ 1) for s in range(count)])


def other_chip(value):
    return lax.ppermute(value, "rep", [(r, r ^ 2) for r in range(4)])


def other_core(value):
    return lax.ppermute(value, "rep", [(r, r ^ 1) for r in range(4)])


def crossed(even_value, odd_value, even_pair, odd_pair):
    value = jnp.where(lax.axis_index("rep") % 2 == 0, even_value, odd_value)
    reps = lax.axis_size("rep")
    pairs = []
    for s in range(lax.axis_size("shard")):
        for r in range(reps):
            to_shard, to_rep = (even_pair if r % 2 == 0 else odd_pair)(s, r)
            pairs.append((s * reps + r, to_shard * reps + to_rep))
    return lax.ppermute(value, ("shard", "rep"), pairs)


def gather_rows(own):
    count = lax.axis_size("shard")
    below = along_z(own, 1)
    above = along_z(own, -1)
    mirror = mirror_y(own)
    far = crossed(
        below,
        above,
        lambda s, r: ((s + LINES) % count, r),
        lambda s, r: ((s - LINES) % count, r),
    )
    mirror, _ = lax.optimization_barrier((mirror, far))
    mirror_below = along_z(mirror, 1)
    mirror_above = along_z(mirror, -1)
    mirror_far = mirror_y(far)
    return ((own, below, above, far), (mirror, mirror_below, mirror_above, mirror_far))


def gather_weights(own):
    across = other_chip(own)
    pair = next_y(own)
    beside = other_core(own)
    pair_beside = other_core(pair)
    across_beside = other_core(across)
    pair_across = crossed(
        pair, across, lambda s, r: (s, r ^ 2), lambda s, r: (s ^ 1, r)
    )
    pair_across_beside = other_core(pair_across)
    return (
        (own, beside, across, across_beside),
        (pair, pair_beside, pair_across, pair_across_beside),
    )


def after(value, *others):
    return lax.optimization_barrier((value,) + others)[0]


def slot_columns(rows, rep_index):
    width = rows.shape[1] // 4
    return jnp.concatenate(
        [lax.dynamic_slice_in_dim(rows, (rep_index ^ j) * width, width, 1) for j in range(4)], axis=1
    )


def owner_order(shard_index):
    line_z = shard_index // LINES
    high = (shard_index // 2) % 2
    steps = jnp.array([0, -1, 1, 2], jnp.int32)
    owners = jnp.mod(line_z + steps, 4) * 2
    low_first = (1 - shard_index % 2).reshape(1)
    return owners + high, owners + 1 - high, low_first.astype(jnp.int32)


def to_owners(ordered):
    lines = lax.axis_size("shard") // LINES
    groups = [
        [z * LINES + y for z in range(lines) for y in (0, 3)],
        [z * LINES + y for z in range(lines) for y in (1, 2)],
    ]
    return lax.all_to_all(
        ordered, "shard", split_axis=0, concat_axis=0, axis_index_groups=groups, tiled=True
    )


def hadamard_pair():
    modulus = FACTOR_A // 2 - 1
    residues = jnp.arange(modulus, dtype=jnp.int32)
    squares = jnp.arange(1, modulus, dtype=jnp.int32) ** 2 % modulus
    differ = (residues[None, :] - residues[:, None]) % modulus
    residue_mask = jnp.any(differ[:, :, None] == squares[None, None, :], axis=2)
    jacobs = jnp.where(differ == 0, 0.0, jnp.where(residue_mask, 1.0, -1.0)).astype(jnp.float32)
    top_row = jnp.concatenate(
        [jnp.zeros((1, 1), jnp.float32), jnp.ones((1, modulus), jnp.float32)], axis=1
    )
    lower_rows = jnp.concatenate([-jnp.ones((modulus, 1), jnp.float32), jacobs], axis=1)
    paley_core = jnp.eye(modulus + 1, dtype=jnp.float32) + jnp.concatenate(
        [top_row, lower_rows], axis=0
    )
    doubler = jnp.array([[1.0, 1.0], [1.0, -1.0]], jnp.float32)
    outer_factor = jnp.kron(doubler, paley_core)
    indices = jnp.arange(FACTOR_B, dtype=jnp.int32)
    common_bits = indices[:, None] & indices[None, :]
    parity = jnp.zeros((FACTOR_B, FACTOR_B), jnp.int32)
    for bit_level in range(FACTOR_B.bit_length() - 1):
        parity = parity + (common_bits >> bit_level & 1)
    inner_factor = (1 - 2 * (parity % 2)).astype(jnp.float32)
    return (outer_factor, inner_factor)


def rotate_column_part(matrix, part_index, part_total):
    outer_factor, inner_factor = hadamard_pair()
    height = matrix.shape[0]
    blocks = matrix.reshape(height, FACTOR_A, FACTOR_B)
    inner_mixed = jnp.einsum(
        "mab,by->may", blocks, inner_factor.astype(jnp.bfloat16), preferred_element_type=jnp.float32
    )
    part_width = FACTOR_A // part_total
    outer_part = lax.dynamic_slice_in_dim(outer_factor, part_index * part_width, part_width, 1)
    outer_part = jnp.concatenate(
        [
            lax.dynamic_slice_in_dim(outer_part, (part_index ^ j) * part_width, part_width, 0)
            for j in range(part_total)
        ],
        axis=0,
    )
    turned = jnp.einsum("may,ax->mxy", inner_mixed, outer_part, precision=lax.Precision.HIGHEST)
    return (turned.reshape(height, part_width * FACTOR_B) * (1.0 / math.sqrt(D))).astype(jnp.bfloat16)


def rotate_columns(matrix):
    outer_factor, inner_factor = hadamard_pair()
    height = matrix.shape[0]
    blocks = matrix.reshape(height, FACTOR_A, FACTOR_B)
    inner_mixed = jnp.einsum(
        "mab,by->may", blocks, inner_factor.astype(jnp.bfloat16), preferred_element_type=jnp.float32
    )
    turned = jnp.einsum("may,ax->mxy", inner_mixed, outer_factor, precision=lax.Precision.HIGHEST)
    return (turned.reshape(height, D) * (1.0 / math.sqrt(D))).astype(jnp.bfloat16)


def normalize(states, gain):
    mean_square = jnp.mean(states * states, axis=-1, keepdims=True)
    return (states * lax.rsqrt(mean_square + EPSILON) * gain.astype(jnp.float32)).astype(
        jnp.bfloat16
    )


def spun(vectors, cosine, sine):
    return vectors * cosine + pltpu.roll(vectors, HEAD_DIM // 2, 1) * sine


def attention_kernel(
    part_ref, length_ref, packed_ref, cosine_ref, sine_ref, keys_ref, values_ref, out_ref, spun_ref, sum_ref
):
    block = pl.program_id(0)
    group = part_ref[0] ^ pl.program_id(1)
    cached = keys_ref.shape[1]
    rows = keys_ref.shape[0]
    tokens = rows * STEPS
    piece_heads = packed_ref.shape[2] // HEAD_DIM
    ratio = HEADS // KV_HEADS
    cosine = cosine_ref[...]
    sine = sine_ref[...]

    def head(index):
        offset = pl.multiple_of(lax.rem(index, piece_heads) * HEAD_DIM, HEAD_DIM)
        return packed_ref[index // piece_heads, :, pl.ds(offset, HEAD_DIM)]

    for u in range(2 * ratio):
        turned = spun(head(group * 2 * ratio + u).astype(jnp.float32), cosine, sine)
        spun_ref[:, u * HEAD_DIM : (u + 1) * HEAD_DIM] = turned.astype(jnp.bfloat16).astype(jnp.float32)
    scale = 1.0 / math.sqrt(HEAD_DIM)
    pairs = rows // 2
    group_rows = 2 * STEPS * ratio
    count = pairs * group_rows
    place = lax.broadcasted_iota(jnp.int32, (count, 1), 0)
    token_of = (place // group_rows) * (2 * STEPS) + place % (2 * STEPS)
    row_of = token_of // STEPS
    live = jnp.zeros((count, 1), jnp.int32)
    for row in range(rows):
        live = jnp.where(row_of == row, length_ref[block * rows + row], live)
    old_start = (row_of % 2) * cached
    old_column = lax.broadcasted_iota(jnp.int32, (count, 2 * cached), 1) - old_start
    old_kept = (old_column >= 0) & (old_column < live)
    new_column = lax.broadcasted_iota(jnp.int32, (count, tokens), 1)
    new_kept = (new_column >= row_of * STEPS) & (new_column <= token_of)
    contract_last = (((1,), (1,)), ((), ()))

    def columns(half, u):
        return slice((half * ratio + u) * HEAD_DIM, (half * ratio + u + 1) * HEAD_DIM)

    for half in range(2):
        lanes = slice(half * HEAD_DIM, (half + 1) * HEAD_DIM)
        new_keys = spun(head(HEADS + group * 2 + half).astype(jnp.float32), cosine, sine).astype(jnp.bfloat16)
        new_values = head(HEADS + KV_HEADS + group * 2 + half)
        queries = [
            jnp.concatenate(
                [spun_ref[2 * STEPS * pair : 2 * STEPS * (pair + 1), columns(half, u)] for u in range(ratio)],
                axis=0,
            )
            for pair in range(pairs)
        ]
        old_scores = jnp.concatenate(
            [
                lax.dot_general(
                    queries[pair].astype(jnp.bfloat16),
                    keys_ref[2 * pair : 2 * pair + 2, :, lanes].reshape(2 * cached, HEAD_DIM),
                    contract_last,
                    preferred_element_type=jnp.float32,
                )
                for pair in range(pairs)
            ],
            axis=0,
        )
        new_scores = lax.dot_general(
            jnp.concatenate(queries, axis=0).astype(jnp.bfloat16),
            new_keys,
            contract_last,
            preferred_element_type=jnp.float32,
        )
        old_scores = jnp.where(old_kept, old_scores * scale, -1e30)
        new_scores = jnp.where(new_kept, new_scores * scale, -1e30)
        peak = jnp.maximum(
            jnp.max(old_scores, axis=1, keepdims=True), jnp.max(new_scores, axis=1, keepdims=True)
        )
        old_exp = jnp.exp(old_scores - peak)
        new_exp = jnp.exp(new_scores - peak)
        share = 1.0 / (jnp.sum(old_exp, axis=1, keepdims=True) + jnp.sum(new_exp, axis=1, keepdims=True))
        old_weights = old_exp * share
        fresh = jnp.dot(
            (new_exp * share).astype(jnp.bfloat16), new_values, preferred_element_type=jnp.float32
        )
        for pair in range(pairs):
            part = slice(pair * group_rows, (pair + 1) * group_rows)
            total = fresh[part] + jnp.dot(
                old_weights[part].astype(jnp.bfloat16),
                values_ref[2 * pair : 2 * pair + 2, :, lanes].reshape(2 * cached, HEAD_DIM),
                preferred_element_type=jnp.float32,
            )
            for u in range(ratio):
                sum_ref[2 * STEPS * pair : 2 * STEPS * (pair + 1), columns(half, u)] = total[
                    2 * STEPS * u : 2 * STEPS * (u + 1)
                ]
    out_ref[...] = sum_ref[...].astype(jnp.bfloat16)


def attend_slots(pieces, keys, values, lengths, rep_index):
    rows, cached = keys.shape[0], keys.shape[1]
    block_rows = 8
    tokens = block_rows * STEPS
    positions = (lengths[:, None] + jnp.arange(STEPS, dtype=jnp.int32)[None, :]).reshape(-1)
    frequency = jnp.power(
        jnp.float32(ROPE_BASE), -jnp.arange(0, HEAD_DIM, 2, dtype=jnp.float32) / HEAD_DIM
    )
    angles = positions.astype(jnp.float32)[:, None] * frequency[None, :]
    cosine, sine = jnp.cos(angles), jnp.sin(angles)
    cosine = jnp.concatenate([cosine, cosine], axis=1)
    sine = jnp.concatenate([-sine, sine], axis=1)
    width = QDIM // 4
    pair_width = KVD // 4
    return pl.pallas_call(
        attention_kernel,
        out_shape=jax.ShapeDtypeStruct((rows * STEPS, QDIM), jnp.bfloat16),
        grid_spec=pltpu.PrefetchScalarGridSpec(
            num_scalar_prefetch=2,
            grid=(rows // block_rows, 4),
            in_specs=[
                pl.BlockSpec((pieces.shape[0], tokens, pieces.shape[2]), lambda i, j, p, n: (0, i, 0)),
                pl.BlockSpec((tokens, HEAD_DIM), lambda i, j, p, n: (i, 0)),
                pl.BlockSpec((tokens, HEAD_DIM), lambda i, j, p, n: (i, 0)),
                pl.BlockSpec((block_rows, cached, pair_width), lambda i, j, p, n: (i, 0, p[0] ^ j)),
                pl.BlockSpec((block_rows, cached, pair_width), lambda i, j, p, n: (i, 0, p[0] ^ j)),
            ],
            out_specs=pl.BlockSpec((tokens, width), lambda i, j, p, n: (i, j)),
            scratch_shapes=[
                pltpu.VMEM((tokens, width), jnp.float32),
                pltpu.VMEM((tokens, width), jnp.float32),
            ],
        ),
        cost_estimate=pl.CostEstimate(flops=2_000_000_000, bytes_accessed=10_000_000, transcendentals=2_000_000),
        name="attend_slots",
    )(rep_index.astype(jnp.int32).reshape(1), lengths, pieces, cosine, sine, keys, values)


def product_kernel(blocks, groups, has_other, has_buffer, order_ref, *refs):
    refs = list(refs)
    row_refs = [refs.pop(0) for _ in range(blocks)]
    weight_refs = [refs.pop(0) for _ in range(4 * groups)]
    bias_ref = refs.pop(0)
    other_ref = refs.pop(0) if has_other else None
    if has_buffer:
        refs.pop(0)
    out_ref, rows_vmem, weights_vmem, total, out_vmem, row_sem, weight_sem, out_sem = refs
    height = row_refs[0].shape[0]
    _, depth = weight_refs[0].shape

    def row_copy(m, j):
        columns = pl.ds(j * depth, depth) if isinstance(j, int) else pl.ds(pl.multiple_of(j * depth, depth), depth)
        return pltpu.make_async_copy(
            row_refs[m].at[:, columns],
            rows_vmem.at[pl.ds(m * height, height), columns],
            row_sem.at[m, j],
        )

    def weight_copy(i):
        return pltpu.make_async_copy(weight_refs[i], weights_vmem.at[i], weight_sem.at[i])

    for j in range(4):
        weight_copy(j).start()
        for m in range(blocks):
            row_copy(m, j).start()
    for i in range(4, 4 * groups):
        weight_copy(i).start()
    total[...] = jnp.zeros_like(total)

    @pl.loop(0, 4 * groups)
    def _(i):
        pltpu.make_async_copy(weight_refs[0], weights_vmem.at[i], weight_sem.at[i]).wait()

        @pl.when(i < 4)
        def _():
            for m in range(blocks):
                row_copy(m, i).wait()

        columns = pl.ds(pl.multiple_of(lax.rem(i, 4) * depth, depth), depth)
        total[i // 4] += lax.dot_general(
            rows_vmem[:, columns],
            weights_vmem[i],
            (((1,), (1,)), ((), ())),
            preferred_element_type=jnp.float32,
        )

    if groups == 1 and not has_other:
        out_ref[...] = (total[0] + bias_ref[...]).astype(jnp.bfloat16)
        return
    low_first = order_ref[blocks] == 1
    if has_other:
        mine = other_ref[...].astype(jnp.float32)
        others = total[0] + bias_ref[...]
    else:
        mine = total[0]
        others = total[1]

    @pl.when(low_first)
    def _():
        out_vmem[...] = jnp.concatenate([mine, others], axis=1).astype(jnp.bfloat16)

    @pl.when(jnp.logical_not(low_first))
    def _():
        out_vmem[...] = jnp.concatenate([others, mine], axis=1).astype(jnp.bfloat16)

    out_copies = [
        pltpu.make_async_copy(out_vmem.at[pl.ds(m * height, height)], out_ref.at[order_ref[m]], out_sem.at[m])
        for m in range(blocks)
    ]
    for copy in out_copies:
        copy.start()
    for copy in out_copies:
        copy.wait()


def product(row_blocks, weights, bias, order, other=None, buffer=None, partial=False):
    blocks = len(row_blocks)
    groups = len(weights) // 4
    height, full = row_blocks[0].shape
    width, depth = weights[0].shape
    anywhere = pl.BlockSpec(memory_space=pl.ANY)
    inside = pl.BlockSpec(memory_space=pltpu.VMEM)
    operands = list(row_blocks) + list(weights) + [bias]
    specs = [anywhere] * (len(operands) - 1) + [inside]
    if other is not None:
        operands.append(other)
        specs.append(inside)
    aliases = {}
    if buffer is not None:
        operands.append(buffer)
        specs.append(anywhere)
        aliases = {len(operands): 0}
    if partial:
        out_shape = jax.ShapeDtypeStruct((blocks * height, width), jnp.bfloat16)
    else:
        out_shape = jax.ShapeDtypeStruct((8, height, 2 * width), jnp.bfloat16)
    return pl.pallas_call(
        functools.partial(product_kernel, blocks, groups, other is not None, buffer is not None),
        out_shape=out_shape,
        grid_spec=pltpu.PrefetchScalarGridSpec(
            num_scalar_prefetch=1,
            grid=(),
            in_specs=specs,
            out_specs=inside if partial else anywhere,
            scratch_shapes=[
                pltpu.VMEM((blocks * height, full), jnp.bfloat16),
                pltpu.VMEM((4 * groups, width, depth), jnp.bfloat16),
                pltpu.VMEM((groups, blocks * height, width), jnp.float32),
                pltpu.VMEM((blocks * height, 2 * width), jnp.bfloat16),
                pltpu.SemaphoreType.DMA((blocks, 4)),
                pltpu.SemaphoreType.DMA((4 * groups,)),
                pltpu.SemaphoreType.DMA((blocks,)),
            ],
        ),
        input_output_aliases=aliases,
        cost_estimate=pl.CostEstimate(
            flops=2 * blocks * height * full * width * groups,
            bytes_accessed=2 * full * width * groups + 2 * blocks * height * full,
            transcendentals=0,
        ),
        name="product",
    )(order, *operands)


def body(qkv_versions, qkv_bias, o_versions, norm_gain, hidden, cache_keys, cache_values, lengths):
    trainer_side = lax.axis_index("role") == 0
    shard_index = lax.axis_index("shard")
    rep_index = lax.axis_index("rep")
    rep_total = lax.axis_size("rep")
    own_qkv = qkv_versions[0].T
    own_out = o_versions[0]
    states = hidden[0].astype(jnp.float32)
    rows = states.shape[0]
    tokens = rows * STEPS
    near, far, low_first = owner_order(shard_index)
    normed = normalize(states, norm_gain[0]).reshape(tokens, D)
    qkv_slots = gather_weights(own_qkv)
    width = own_qkv.shape[0]
    bias = qkv_bias[0].astype(jnp.float32).reshape(1, -1)
    own_bias = lax.dynamic_slice_in_dim(bias, shard_index * width, width, 1)
    pair_bias = lax.dynamic_slice_in_dim(bias, (shard_index ^ 1) * width, width, 1)
    same, mirror = gather_rows(slot_columns(normed, rep_index))
    order = jnp.concatenate([near, far, low_first])
    folded_qkv = rotate_column_part(
        after(jnp.concatenate(qkv_slots[0], axis=1), same[3]), rep_index, rep_total
    )
    mine = product(same + mirror, qkv_slots[0], own_bias, after(order, folded_qkv), partial=True)
    part = product(same + mirror, qkv_slots[1], pair_bias, order, other=mine)
    packed = to_owners(part)
    spread = lax.all_to_all(
        after(own_out, part), "shard", split_axis=0, concat_axis=1, tiled=True
    )
    out_slots = gather_weights(after(own_out.T, qkv_slots[1][2]))
    attended = attend_slots(packed, cache_keys[0], cache_values[0], lengths[0], rep_index)
    same, mirror = gather_rows(attended)
    weights = out_slots[0] + out_slots[1]
    no_bias = jnp.zeros((1, own_out.shape[1]), jnp.float32)
    part = product(same, weights, no_bias, jnp.concatenate([near, low_first]))
    turned = after(rotate_columns(after(spread, attended)), part)
    folded_out = lax.all_to_all(turned, "shard", split_axis=1, concat_axis=0, tiled=True)
    part = product(mirror, weights, no_bias, jnp.concatenate([far, low_first]), buffer=part)
    projected = to_owners(part)
    projected = projected.transpose(1, 0, 2).reshape(rows, STEPS, D).astype(jnp.float32)
    layer_out = (states + projected).astype(jnp.bfloat16)[None]
    sent_qkv, sent_out = shifted((folded_qkv, folded_out), "role", 1)
    new_qkv = jnp.where(trainer_side, folded_qkv, sent_qkv)
    new_o = jnp.where(trainer_side, folded_out, sent_out)
    return (layer_out, new_qkv.T[None], new_o[None])


def solution(mesh):
    in_specs = (
        P("role", "rep", "shard"),
        P("role", None),
        P("role", "rep", "shard"),
        P("role", None),
        P("role", ("shard", "rep"), None, None),
        P("role", ("shard", "rep"), None, None),
        P("role", ("shard", "rep"), None, None),
        P("role", ("shard", "rep")),
    )
    out_specs = (
        P("role", ("shard", "rep"), None, None),
        P("role", "rep", "shard"),
        P("role", "rep", "shard"),
    )
    return jax.shard_map(body, mesh=mesh, in_specs=in_specs, out_specs=out_specs, check_vma=False)
```

profile of v0, /device:TPU:0, one launch (start us, length us, event | category | flops | bytes accessed | tf_op | source)
XLA Modules:
  0.0 252.4 jit_solution(15575413246237037842)
XLA Ops:
  0.7 1.5 reshape.171
  3.1 2.1 collective-permute-start
  5.2 2.2 collective-permute-start.1
  7.4 1.5 collective-permute-start.9
  8.9 3.0 %collective-permute-start.3 = (bf16[64,5120]{1,0:T(8,128)(2,1)S(1)}, bf16[64,5120]{1,0:T(8,128)(2,1)}, u32[]{:S(2)}, u32[]{:S(2)}) collective-permute-start(bf16[64,5120]{1,0:T(8,128)(2,1)S(1)} %pad_maximum_fusion.1.refs_0_), channel_id=1, source_target_pairs={{0,12},{4,8},{8,4},{12,0},{16,28},{20,24},{24,20},{28,16},{32,44},... | collective-permute-start | bytes 1966088 | tf_op jit(solution)/shard_map/ppermute | solution.py:44
  12.7 9.4 %collective-permute-done.refs_1_ = bf16[64,5120]{1,0:T(8,128)(2,1)S(1)} collective-permute-done((bf16[64,5120]{1,0:T(8,128)(2,1)S(1)}, bf16[64,5120]{1,0:T(8,128)(2,1)S(1)}, u32[]{:S(2)}, u32[]{:S(2)}) %collective-permute-start) | collective-permute-done | bytes 655392 | tf_op jit(solution)/shard_map/ppermute | solution.py:39
  22.1 1.6 collective-permute-start.7
  23.8 10.5 %collective-permute-done.9.refs_10_ = bf16[448,1280]{1,0:T(8,128)(2,1)S(1)} collective-permute-done((bf16[448,1280]{1,0:T(8,128)(2,1)}, bf16[448,1280]{1,0:T(8,128)(2,1)S(1)}, u32[]{:S(2)}, u32[]{:S(2)}) %collective-permute-start.9) | collective-permute-done | bytes 1146912 | tf_op jit(solution)/shard_map/ppermute | solution.py:53
  34.4 14.6 %collective-permute-done.7.refs_8_ = bf16[448,1280]{1,0:T(8,128)(2,1)} collective-permute-done((bf16[448,1280]{1,0:T(8,128)(2,1)}, bf16[448,1280]{1,0:T(8,128)(2,1)}, u32[]{:S(2)}, u32[]{:S(2)}) %collective-permute-start.7) | collective-permute-done | bytes 1146912 | tf_op jit(solution)/shard_map/ppermute | solution.py:49
  48.9 1.4 broadcast_select_fusion
  50.4 1.6 collective-permute-start.10
  52.6 0.7 constant_dynamic-slice_fusion
  53.5 3.2 %collective-permute-start.5 = (bf16[64,5120]{1,0:T(8,128)(2,1)}, bf16[64,5120]{1,0:T(8,128)(2,1)}, u32[]{:S(2)}, u32[]{:S(2)}) collective-permute-start(bf16[64,5120]{1,0:T(8,128)(2,1)} %collective-permute-done.3.refs_4_), channel_id=1, source_target_pairs={{0,48},{4,52},{8,56},{12,60},{16,0},{20,4},{24,8},{28,12},{32,16},... | collective-permute-start | bytes 1966088 | tf_op jit(solution)/shard_map/ppermute | solution.py:39
  56.7 3.0 %collective-permute-start.6 = (bf16[64,5120]{1,0:T(8,128)(2,1)}, bf16[64,5120]{1,0:T(8,128)(2,1)}, u32[]{:S(2)}, u32[]{:S(2)}) collective-permute-start(bf16[64,5120]{1,0:T(8,128)(2,1)} %collective-permute-done.2.refs_3_), channel_id=1, source_target_pairs={{0,12},{4,8},{8,4},{12,0},{16,28},{20,24},{24,20},{28,16},{32,44},... | collective-permute-start | bytes 1966088 | tf_op jit(solution)/shard_map/ppermute | solution.py:44
  59.7 1.9 pad_maximum_fusion
  61.6 1.2 copy.56
  62.9 3.5 %collective-permute-done.10.refs_10_ = bf16[448,1280]{1,0:T(8,128)(2,1)} collective-permute-done((bf16[448,1280]{1,0:T(8,128)(2,1)S(1)}, bf16[448,1280]{1,0:T(8,128)(2,1)}, u32[]{:S(2)}, u32[]{:S(2)}) %collective-permute-start.10) | collective-permute-done | bytes 1146912 | tf_op jit(solution)/shard_map/ppermute | solution.py:68
  66.4 2.6 %fusion.9 = f32[448,40,128]{2,1,0:T(8,128)S(1)} fusion(bf16[448,40,128]{2,1,0:T(8,128)(2,1)S(1)} %bitcast.56), kind=kOutput, calls=%fused_computation.31 | convolution fusion | flops 587792384 | bytes 13762560 | tf_op jit(solution)/shard_map/mab,by->may/dot_general | solution.py:165
  69.0 5.0 %fusion = bf16[448,10,128]{2,1,0:T(8,128)(2,1)S(1)} fusion(f32[448,40,128]{2,1,0:T(8,128)S(1)} %fusion.9, f32[10,10]{0,1:T(8,128)S(1)} %get-tuple-element.40, f32[10,10]{0,1:T(8,128)S(1)} %get-tuple-element.41, f32[10,10]{0,1:T(8,128)S(1)} %get-tuple-element.42, f32[10,10]{0,1:T(8,128)S(1)} %get-tuple-element.39), kind=kOutput, calls=%fused_computation.3 | convolution fusion | flops 276399296 | bytes 10323520 | tf_op jit(solution)/shard_map/may,ax->mxy/dot_general | solution.py:177
  74.0 1.8 copy.45
  75.9 8.9 %product.4.refs_13_ = bf16[512,448]{1,0:T(8,128)(2,1)} custom-call(s32[9]{0:T(128)} %pad_add_fusion.1.order_ref, bf16[64,5120]{1,0:T(8,128)(2,1)} %copy-done.3, bf16[64,5120]{1,0:T(8,128)(2,1)} %copy-done.4, bf16[64,5120]{1,0:T(8,128)(2,1)} %copy-done.5, bf16[64,5120]{1,0:T(8,128)(2,1)} %collective-permute-done.2.refs_3_, ...), custom_call_target="tpu_custom_call" | custom-call | flops 2348810240 | bytes 9830400 | tf_op jit(solution)/shard_map/product/pallas_call | solution.py:434
  84.8 9.6 %product.5 = bf16[8,64,896]{2,1,0:T(8,128)(2,1)} custom-call(s32[9]{0:T(128)} %pad_add_fusion.1.order_ref, bf16[64,5120]{1,0:T(8,128)(2,1)} %copy-done.3, bf16[64,5120]{1,0:T(8,128)(2,1)} %copy-done.4, bf16[64,5120]{1,0:T(8,128)(2,1)} %copy-done.5, bf16[64,5120]{1,0:T(8,128)(2,1)} %collective-permute-done.2.refs_3_, ...), custom_call_target="tpu_custom_call" | custom-call | flops 2348810240 | bytes 9830400 | tf_op jit(solution)/shard_map/product/pallas_call | solution.py:434
  94.4 5.3 %all-to-all-start = ((bf16[8,64,896]{2,1,0:T(8,128)(2,1)}), bf16[8,64,896]{2,1,0:T(8,128)(2,1)}, u32[]{:S(2)}, u32[]{:S(2)}) async-start(bf16[8,64,896]{2,1,0:T(8,128)(2,1)} %product.5), calls=%async_computation | async-start | bytes 1835008 | tf_op jit(solution)/shard_map/all_to_all | solution.py:131
  99.8 1.6 collective-permute-start.22
  102.3 0.7 pad_maximum_fusion.2
  103.0 13.1 %all-to-all-done.packed_ref = bf16[8,64,896]{2,1,0:T(8,128)(2,1)} async-done(((bf16[8,64,896]{2,1,0:T(8,128)(2,1)}), bf16[8,64,896]{2,1,0:T(8,128)(2,1)}, u32[]{:S(2)}, u32[]{:S(2)}) %all-to-all-start) | async-done | bytes 917536 | tf_op jit(solution)/shard_map/all_to_all | solution.py:131
  116.1 12.3 %attend_slots.1.refs_0_ = bf16[64,5120]{1,0:T(8,128)(2,1)} custom-call(s32[1]{0:T(128)} %bitcast.1.part_ref, s32[16]{0:T(128)} %bitcast.73, bf16[8,64,896]{2,1,0:T(8,128)(2,1)} %all-to-all-done.packed_ref, f32[64,128]{1,0:T(8,128)} %get-tuple-element.46.cosine_ref, f32[64,128]{1,0:T(8,128)} %get-tuple-element.47.sine_ref, bf16[16,128,1024]{2,1,0:T(8,128)(2,1)} %bitcast.65, ...), custom_call_target="tpu_custom_call" | custom-call | flops 2000000000 | bytes 10000000 | tf_op jit(solution)/shard_map/attend_slots/pallas_call | solution.py:312
  128.4 3.2 %collective-permute-start.16 = (bf16[64,5120]{1,0:T(8,128)(2,1)}, bf16[64,5120]{1,0:T(8,128)(2,1)}, u32[]{:S(2)}, u32[]{:S(2)}) collective-permute-start(bf16[64,5120]{1,0:T(8,128)(2,1)} %attend_slots.1.refs_0_), channel_id=1, source_target_pairs={{0,48},{4,52},{8,56},{12,60},{16,0},{20,4},{24,8},{28,12},{32,16},... | collective-permute-start | bytes 1966088 | tf_op jit(solution)/shard_map/ppermute | solution.py:39
  131.7 2.4 broadcast_select_fusion.1
  134.1 1.5 collective-permute-start.26
  135.6 1.3 copy.49
  136.9 4.3 %all-to-all-start.2 = ((bf16[16,80,320]{2,1,0:T(8,128)(2,1)}), bf16[16,80,320]{2,1,0:T(8,128)(2,1)}, u32[]{:S(2)}, u32[]{:S(2)}) async-start(bf16[16,80,320]{2,1,0:T(8,128)(2,1)} %bitcast.67), calls=%async_computation.2 | async-start | bytes 1966080 | tf_op jit(solution)/shard_map/all_to_all | solution.py:487
  141.2 3.0 %collective-permute-start.14 = (bf16[64,5120]{1,0:T(8,128)(2,1)}, bf16[64,5120]{1,0:T(8,128)(2,1)}, u32[]{:S(2)}, u32[]{:S(2)}) collective-permute-start(bf16[64,5120]{1,0:T(8,128)(2,1)} %attend_slots.1.refs_0_), channel_id=1, source_target_pairs={{0,12},{4,8},{8,4},{12,0},{16,28},{20,24},{24,20},{28,16},{32,44},... | collective-permute-start | bytes 1966088 | tf_op jit(solution)/shard_map/ppermute | solution.py:44
  144.2 11.6 %collective-permute-done.15.refs_1_ = bf16[64,5120]{1,0:T(8,128)(2,1)} collective-permute-done((bf16[64,5120]{1,0:T(8,128)(2,1)}, bf16[64,5120]{1,0:T(8,128)(2,1)}, u32[]{:S(2)}, u32[]{:S(2)}) %collective-permute-start.15) | collective-permute-done | bytes 655392 | tf_op jit(solution)/shard_map/ppermute | solution.py:39
  155.9 2.0 broadcast_select_fusion.2
  158.5 7.2 %collective-permute-done.14.refs_0_ = bf16[64,5120]{1,0:T(8,128)(2,1)} collective-permute-done((bf16[64,5120]{1,0:T(8,128)(2,1)}, bf16[64,5120]{1,0:T(8,128)(2,1)}, u32[]{:S(2)}, u32[]{:S(2)}) %collective-permute-start.14) | collective-permute-done | bytes 655392 | tf_op jit(solution)/shard_map/ppermute | solution.py:44
  166.3 1.4 copy.47
  167.8 2.4 copy.50
  170.1 2.6 %all_to_all.39 = bf16[80,5120]{1,0:T(8,128)(2,1)} reshape(bf16[80,16,320]{2,1,0:T(8,128)(2,1)} %copy.50) | data formatting | bytes 1638400 | tf_op jit(solution)/shard_map/all_to_all | solution.py:487
  172.8 1.3 copy.57
  174.1 6.0 %collective-permute-start.28 = (bf16[448,1280]{1,0:T(8,128)(2,1)}, bf16[448,1280]{1,0:T(8,128)(2,1)}, u32[]{:S(2)}, u32[]{:S(2)}) collective-permute-start(bf16[448,1280]{1,0:T(8,128)(2,1)} %copy.47), channel_id=1, source_target_pairs={{0,64},{1,65},{2,66},{3,67},{4,68},{5,69},{6,70},{7,71},{8,72},{9,... | collective-permute-start | bytes 3440648 | tf_op jit(solution)/shard_map/ppermute | solution.py:33
  180.7 1.5 multiply_convert_fusion.1
  182.2 1.0 copy.60
  183.2 1.5 collective-permute-start.18
  184.7 1.8 collective-permute-start.19
  187.5 8.6 %product.6.refs_13_ = bf16[8,64,640]{2,1,0:T(8,128)(2,1)} custom-call(s32[5]{0:T(128)} %pad_add_fusion.2.order_ref, bf16[64,5120]{1,0:T(8,128)(2,1)} %attend_slots.1.refs_0_, bf16[64,5120]{1,0:T(8,128)(2,1)} %collective-permute-done.15.refs_1_, bf16[64,5120]{1,0:T(8,128)(2,1)} %collective-permute-done.16.refs_2_, ...), custom_call_target="tpu_custom_call" | custom-call | flops 1677721600 | bytes 9175040 | tf_op jit(solution)/shard_map/product/pallas_call | solution.py:434
  196.1 0.8 all_to_all.40
  196.9 1.2 copy.51
  198.1 5.4 %all-to-all-start.3 = ((bf16[80,16,320]{2,0,1:T(8,128)(2,1)}), bf16[80,16,320]{2,0,1:T(8,128)(2,1)S(1)}, u32[]{:S(2)}, u32[]{:S(2)}) async-start(bf16[80,16,320]{2,0,1:T(8,128)(2,1)} %copy.51), calls=%async_computation.3 | async-start | bytes 1966080 | tf_op jit(solution)/shard_map/all_to_all | solution.py:497
  204.5 2.5 copy.48
  207.0 8.5 %product.7 = bf16[8,64,640]{2,1,0:T(8,128)(2,1)} custom-call(s32[5]{0:T(128)} %pad_add_fusion.order_ref, bf16[64,5120]{1,0:T(8,128)(2,1)} %collective-permute-done.14.refs_0_, bf16[64,5120]{1,0:T(8,128)(2,1)} %collective-permute-done.18.refs_1_, bf16[64,5120]{1,0:T(8,128)(2,1)} %collective-permute-done.19.refs_2_, ...), custom_call_target="tpu_custom_call", output_to_operand_aliasing={{}: (14, {})} | custom-call | flops 1677721600 | bytes 9175040 | tf_op jit(solution)/shard_map/product/pallas_call | solution.py:434
  215.5 4.4 %all-to-all-done.3 = bf16[80,16,320]{2,0,1:T(8,128)(2,1)S(1)} async-done(((bf16[80,16,320]{2,0,1:T(8,128)(2,1)}), bf16[80,16,320]{2,0,1:T(8,128)(2,1)S(1)}, u32[]{:S(2)}, u32[]{:S(2)}) %all-to-all-start.3) | async-done | bytes 819232 | tf_op jit(solution)/shard_map/all_to_all | solution.py:497
  219.8 3.5 %all-to-all-start.1 = ((bf16[8,64,640]{2,1,0:T(8,128)(2,1)}), bf16[8,64,640]{2,1,0:T(8,128)(2,1)S(1)}, u32[]{:S(2)}, u32[]{:S(2)}) async-start(bf16[8,64,640]{2,1,0:T(8,128)(2,1)} %product.7), calls=%async_computation.1 | async-start | bytes 1310720 | tf_op jit(solution)/shard_map/all_to_all | solution.py:131
  223.4 1.4 select_bitcast_fusion
  224.8 2.4 copy.54
  227.2 1.3 copy.52
  228.4 4.4 %collective-permute-start.29 = (bf16[1280,320]{0,1:T(8,128)(2,1)}, bf16[1280,320]{0,1:T(8,128)(2,1)}, u32[]{:S(2)}, u32[]{:S(2)}) collective-permute-start(bf16[1280,320]{0,1:T(8,128)(2,1)} %copy.52), channel_id=1, source_target_pairs={{0,64},{1,65},{2,66},{3,67},{4,68},{5,69},{6,70},{7,71},{8,72},{9,... | collective-permute-start | bytes 2457608 | tf_op jit(solution)/shard_map/ppermute | solution.py:33
  232.9 1.2 all-to-all-done.1
  234.2 1.8 copy.46
  236.0 2.8 %reshape.173 = f32[1,16,4,5120]{3,2,1,0:T(4,128)} reshape(f32[64,8,640]{2,1,0:T(8,128)} %copy.46) | data formatting | bytes 2621440 | tf_op jit(solution)/shard_map/convert_element_type | solution.py:500
  238.8 2.5 add_convert_fusion
  241.3 8.0 %collective-permute-done.29 = bf16[1280,320]{0,1:T(8,128)(2,1)} collective-permute-done((bf16[1280,320]{0,1:T(8,128)(2,1)}, bf16[1280,320]{0,1:T(8,128)(2,1)}, u32[]{:S(2)}, u32[]{:S(2)}) %collective-permute-start.29) | collective-permute-done | bytes 819232 | tf_op jit(solution)/shard_map/ppermute | solution.py:33
  249.3 1.5 copy.53
  251.1 1.3 copy.55
  (102 shorter events, 7.7 us)
Async XLA Ops:
  0.6 1.5 copy-start.6
  0.7 2.0 copy-start.11
  3.0 9.3 %copy-start.15 = (f32[1,20]{1,0:T(1,128)S(1)}, f32[1,20]{1,0:T(1,128)}, u32[]{:S(2)}) copy-start(f32[1,20]{1,0:T(1,128)} %constant.197.clone.1) | copy-start | bytes 244
  3.0 9.4 %copy-start.13 = (f32[2,2]{0,1:T(2,128)S(1)}, f32[2,2]{0,1:T(2,128)}, u32[]{:S(2)}) copy-start(f32[2,2]{0,1:T(2,128)} %constant.214.clone) | copy-start | bytes 52
  3.0 9.6 %copy-start.10 = (bf16[1,7168]{1,0:T(2,128)(2,1)S(1)}, bf16[1,7168]{1,0:T(2,128)(2,1)}, u32[]{:S(2)}) copy-start(bf16[1,7168]{1,0:T(2,128)(2,1)} %param.12) | copy-start | bytes 43012
  3.0 9.6 %copy-start.14 = (s32[4]{0:T(128)S(1)}, s32[4]{0:T(128)}, u32[]{:S(2)}) copy-start(s32[4]{0:T(128)} %constant.213.clone) | copy-start | bytes 52
  3.1 47.2 %copy-start.3 = (bf16[64,5120]{1,0:T(8,128)(2,1)}, bf16[64,5120]{1,0:T(8,128)(2,1)S(1)}, u32[]{:S(2)}) copy-start(bf16[64,5120]{1,0:T(8,128)(2,1)S(1)} %pad_maximum_fusion.1.refs_0_) | copy-start | bytes 1966084
  3.1 18.9 %collective-permute-start = (bf16[64,5120]{1,0:T(8,128)(2,1)S(1)}, bf16[64,5120]{1,0:T(8,128)(2,1)S(1)}, u32[]{:S(2)}, u32[]{:S(2)}) collective-permute-start(bf16[64,5120]{1,0:T(8,128)(2,1)S(1)} %pad_maximum_fusion.1.refs_0_), channel_id=1, source_target_pairs={{0,16},{4,20},{8,24},{12,28},{16,32},{20,36},{24,40},{28,44},{32,4... | collective-permute-start | bytes 1966088 | tf_op jit(solution)/shard_map/ppermute | solution.py:39
  5.2 18.4 %collective-permute-start.1 = (bf16[64,5120]{1,0:T(8,128)(2,1)S(1)}, bf16[64,5120]{1,0:T(8,128)(2,1)S(1)}, u32[]{:S(2)}, u32[]{:S(2)}) collective-permute-start(bf16[64,5120]{1,0:T(8,128)(2,1)S(1)} %pad_maximum_fusion.1.refs_0_), channel_id=1, source_target_pairs={{0,48},{4,52},{8,56},{12,60},{16,0},{20,4},{24,8},{28,12},{32,16},... | collective-permute-start | bytes 1966088 | tf_op jit(solution)/shard_map/ppermute | solution.py:39
  7.4 26.9 %collective-permute-start.9 = (bf16[448,1280]{1,0:T(8,128)(2,1)}, bf16[448,1280]{1,0:T(8,128)(2,1)S(1)}, u32[]{:S(2)}, u32[]{:S(2)}) collective-permute-start(bf16[448,1280]{1,0:T(8,128)(2,1)} %bitcast.5.refs_8_), channel_id=1, source_target_pairs={{0,2},{1,3},{2,0},{3,1},{4,6},{5,7},{6,4},{7,5},{8,10},{9,11},{10,... | collective-permute-start | bytes 3440648 | tf_op jit(solution)/shard_map/ppermute | solution.py:53
  8.9 44.6 %collective-permute-start.12 = (bf16[448,1280]{1,0:T(8,128)(2,1)}, bf16[448,1280]{1,0:T(8,128)(2,1)}, u32[]{:S(2)}, u32[]{:S(2)}) collective-permute-start(bf16[448,1280]{1,0:T(8,128)(2,1)} %bitcast.5.refs_8_), channel_id=1, source_target_pairs={{0,1},{1,0},{2,3},{3,2},{4,5},{5,4},{6,7},{7,6},{8,9},{9,8},{10,11... | collective-permute-start | bytes 3440648 | tf_op jit(solution)/shard_map/ppermute | solution.py:57
  8.9 44.4 %collective-permute-start.3 = (bf16[64,5120]{1,0:T(8,128)(2,1)S(1)}, bf16[64,5120]{1,0:T(8,128)(2,1)}, u32[]{:S(2)}, u32[]{:S(2)}) collective-permute-start(bf16[64,5120]{1,0:T(8,128)(2,1)S(1)} %pad_maximum_fusion.1.refs_0_), channel_id=1, source_target_pairs={{0,12},{4,8},{8,4},{12,0},{16,28},{20,24},{24,20},{28,16},{32,44},... | collective-permute-start | bytes 1966088 | tf_op jit(solution)/shard_map/ppermute | solution.py:44
  22.1 28.2 %copy-start.4 = (bf16[64,5120]{1,0:T(8,128)(2,1)}, bf16[64,5120]{1,0:T(8,128)(2,1)S(1)}, u32[]{:S(2)}) copy-start(bf16[64,5120]{1,0:T(8,128)(2,1)S(1)} %collective-permute-done.refs_1_) | copy-start | bytes 1966084
  22.1 26.9 %collective-permute-start.7 = (bf16[448,1280]{1,0:T(8,128)(2,1)}, bf16[448,1280]{1,0:T(8,128)(2,1)}, u32[]{:S(2)}, u32[]{:S(2)}) collective-permute-start(bf16[448,1280]{1,0:T(8,128)(2,1)} %bitcast.5.refs_8_), channel_id=1, source_target_pairs={{0,4},{4,0},{8,12},{12,8},{16,20},{20,16},{24,28},{28,24},{32,36},... | collective-permute-start | bytes 3440648 | tf_op jit(solution)/shard_map/ppermute | solution.py:49
  23.7 26.7 %copy-start.5 = (bf16[64,5120]{1,0:T(8,128)(2,1)}, bf16[64,5120]{1,0:T(8,128)(2,1)S(1)}, u32[]{:S(2)}) copy-start(bf16[64,5120]{1,0:T(8,128)(2,1)S(1)} %collective-permute-done.1.refs_2_) | copy-start | bytes 1966084
  23.8 29.6 %collective-permute-start.2 = (bf16[64,5120]{1,0:T(8,128)(2,1)S(1)}, bf16[64,5120]{1,0:T(8,128)(2,1)}, u32[]{:S(2)}, u32[]{:S(2)}) collective-permute-start(bf16[64,5120]{1,0:T(8,128)(2,1)S(1)} %broadcast_select_fusion.3), channel_id=1, source_target_pairs={{0,16},{1,49},{2,18},{3,51},{4,20},{5,53},{6,22},{7,55},{8,24},{9,... | collective-permute-start | bytes 1966088 | tf_op jit(solution)/shard_map/ppermute | solution.py:68
  34.4 25.4 %copy-start = (bf16[448,1280]{1,0:T(8,128)(2,1)}, bf16[448,1280]{1,0:T(8,128)(2,1)S(1)}, u32[]{:S(2)}) copy-start(bf16[448,1280]{1,0:T(8,128)(2,1)S(1)} %collective-permute-done.9.refs_10_) | copy-start | bytes 3440644
  34.4 22.3 %collective-permute-start.13 = (bf16[448,1280]{1,0:T(8,128)(2,1)S(1)}, bf16[448,1280]{1,0:T(8,128)(2,1)S(1)}, u32[]{:S(2)}, u32[]{:S(2)}) collective-permute-start(bf16[448,1280]{1,0:T(8,128)(2,1)S(1)} %collective-permute-done.9.refs_10_), channel_id=1, source_target_pairs={{0,1},{1,0},{2,3},{3,2},{4,5},{5,4},{6,7},{7,6},{8,9},{9,8},{10,11... | collective-permute-start | bytes 3440648 | tf_op jit(solution)/shard_map/ppermute | solution.py:57
  50.4 16.0 %collective-permute-start.10 = (bf16[448,1280]{1,0:T(8,128)(2,1)S(1)}, bf16[448,1280]{1,0:T(8,128)(2,1)}, u32[]{:S(2)}, u32[]{:S(2)}) collective-permute-start(bf16[448,1280]{1,0:T(8,128)(2,1)S(1)} %broadcast_select_fusion), channel_id=1, source_target_pairs={{0,2},{1,5},{2,0},{3,7},{4,6},{5,1},{6,4},{7,3},{8,10},{9,13},{10,... | collective-permute-start | bytes 3440648 | tf_op jit(solution)/shard_map/ppermute | solution.py:68
  53.3 31.5 %collective-permute-start.8 = (bf16[448,1280]{1,0:T(8,128)(2,1)}, bf16[448,1280]{1,0:T(8,128)(2,1)}, u32[]{:S(2)}, u32[]{:S(2)}) collective-permute-start(bf16[448,1280]{1,0:T(8,128)(2,1)} %collective-permute-done.7.refs_8_), channel_id=1, source_target_pairs={{0,1},{1,0},{2,3},{3,2},{4,5},{5,4},{6,7},{7,6},{8,9},{9,8},{10,11... | collective-permute-start | bytes 3440648 | tf_op jit(solution)/shard_map/ppermute | solution.py:57
  53.4 22.4 %collective-permute-start.4 = (bf16[64,5120]{1,0:T(8,128)(2,1)}, bf16[64,5120]{1,0:T(8,128)(2,1)}, u32[]{:S(2)}, u32[]{:S(2)}) collective-permute-start(bf16[64,5120]{1,0:T(8,128)(2,1)} %collective-permute-done.3.refs_4_), channel_id=1, source_target_pairs={{0,16},{4,20},{8,24},{12,28},{16,32},{20,36},{24,40},{28,44},{32,4... | collective-permute-start | bytes 1966088 | tf_op jit(solution)/shard_map/ppermute | solution.py:39
  53.5 22.4 %collective-permute-start.5 = (bf16[64,5120]{1,0:T(8,128)(2,1)}, bf16[64,5120]{1,0:T(8,128)(2,1)}, u32[]{:S(2)}, u32[]{:S(2)}) collective-permute-start(bf16[64,5120]{1,0:T(8,128)(2,1)} %collective-permute-done.3.refs_4_), channel_id=1, source_target_pairs={{0,48},{4,52},{8,56},{12,60},{16,0},{20,4},{24,8},{28,12},{32,16},... | collective-permute-start | bytes 1966088 | tf_op jit(solution)/shard_map/ppermute | solution.py:39
  56.7 4.9 %copy-start.8 = (bf16[448,1280]{1,0:T(8,128)(2,1)}, bf16[448,1280]{1,0:T(8,128)(2,1)S(1)}, u32[]{:S(2)}) copy-start(bf16[448,1280]{1,0:T(8,128)(2,1)S(1)} %collective-permute-done.13.refs_11_) | copy-start | bytes 3440644
  56.7 19.1 %collective-permute-start.6 = (bf16[64,5120]{1,0:T(8,128)(2,1)}, bf16[64,5120]{1,0:T(8,128)(2,1)}, u32[]{:S(2)}, u32[]{:S(2)}) collective-permute-start(bf16[64,5120]{1,0:T(8,128)(2,1)} %collective-permute-done.2.refs_3_), channel_id=1, source_target_pairs={{0,12},{4,8},{8,4},{12,0},{16,28},{20,24},{24,20},{28,16},{32,44},... | collective-permute-start | bytes 1966088 | tf_op jit(solution)/shard_map/ppermute | solution.py:44
  66.4 18.4 %collective-permute-start.11 = (bf16[448,1280]{1,0:T(8,128)(2,1)}, bf16[448,1280]{1,0:T(8,128)(2,1)}, u32[]{:S(2)}, u32[]{:S(2)}) collective-permute-start(bf16[448,1280]{1,0:T(8,128)(2,1)} %collective-permute-done.10.refs_10_), channel_id=1, source_target_pairs={{0,1},{1,0},{2,3},{3,2},{4,5},{5,4},{6,7},{7,6},{8,9},{9,8},{10,11... | collective-permute-start | bytes 3440648 | tf_op jit(solution)/shard_map/ppermute | solution.py:57
  94.4 5.3 %copy-start.1 = (bf16[1,1280,320]{1,2,0:T(8,128)(2,1)S(1)}, bf16[1,1280,320]{1,2,0:T(8,128)(2,1)}, u32[]{:S(2)}) copy-start(bf16[1,1280,320]{1,2,0:T(8,128)(2,1)} %param.13) | copy-start | bytes 2457604
  94.4 7.4 %copy-start.12 = (s32[1,16]{1,0:T(1,128)S(1)}, s32[1,16]{1,0:T(1,128)}, u32[]{:S(2)}) copy-start(s32[1,16]{1,0:T(1,128)} %param.18) | copy-start | bytes 196
  94.4 21.6 %all-to-all-start = ((bf16[8,64,896]{2,1,0:T(8,128)(2,1)}), bf16[8,64,896]{2,1,0:T(8,128)(2,1)}, u32[]{:S(2)}, u32[]{:S(2)}) async-start(bf16[8,64,896]{2,1,0:T(8,128)(2,1)} %product.5), calls=%async_computation | async-start | bytes 1835008 | tf_op jit(solution)/shard_map/all_to_all | solution.py:131
  99.8 31.9 %collective-permute-start.22 = (bf16[320,1280]{1,0:T(8,128)(2,1)S(1)}, bf16[320,1280]{1,0:T(8,128)(2,1)S(1)}, u32[]{:S(2)}, u32[]{:S(2)}) collective-permute-start(bf16[320,1280]{1,0:T(8,128)(2,1)S(1)} %bitcast.61), channel_id=1, source_target_pairs={{0,2},{1,3},{2,0},{3,1},{4,6},{5,7},{6,4},{7,5},{8,10},{9,11},{10,... | collective-permute-start | bytes 2457608 | tf_op jit(solution)/shard_map/ppermute | solution.py:53
  101.3 30.3 %collective-permute-start.24 = (bf16[320,1280]{1,0:T(8,128)(2,1)S(1)}, bf16[320,1280]{1,0:T(8,128)(2,1)}, u32[]{:S(2)}, u32[]{:S(2)}) collective-permute-start(bf16[320,1280]{1,0:T(8,128)(2,1)S(1)} %bitcast.62), channel_id=1, source_target_pairs={{0,4},{4,0},{8,12},{12,8},{16,20},{20,16},{24,28},{28,24},{32,36},... | collective-permute-start | bytes 2457608 | tf_op jit(solution)/shard_map/ppermute | solution.py:49
  128.4 27.4 %collective-permute-start.15 = (bf16[64,5120]{1,0:T(8,128)(2,1)}, bf16[64,5120]{1,0:T(8,128)(2,1)}, u32[]{:S(2)}, u32[]{:S(2)}) collective-permute-start(bf16[64,5120]{1,0:T(8,128)(2,1)} %attend_slots.1.refs_0_), channel_id=1, source_target_pairs={{0,16},{4,20},{8,24},{12,28},{16,32},{20,36},{24,40},{28,44},{32,4... | collective-permute-start | bytes 1966088 | tf_op jit(solution)/shard_map/ppermute | solution.py:39
  128.4 27.4 %collective-permute-start.16 = (bf16[64,5120]{1,0:T(8,128)(2,1)}, bf16[64,5120]{1,0:T(8,128)(2,1)}, u32[]{:S(2)}, u32[]{:S(2)}) collective-permute-start(bf16[64,5120]{1,0:T(8,128)(2,1)} %attend_slots.1.refs_0_), channel_id=1, source_target_pairs={{0,48},{4,52},{8,56},{12,60},{16,0},{20,4},{24,8},{28,12},{32,16},... | collective-permute-start | bytes 1966088 | tf_op jit(solution)/shard_map/ppermute | solution.py:39
  131.7 26.2 %copy-start.2 = (bf16[320,1280]{1,0:T(8,128)(2,1)}, bf16[320,1280]{1,0:T(8,128)(2,1)S(1)}, u32[]{:S(2)}) copy-start(bf16[320,1280]{1,0:T(8,128)(2,1)S(1)} %collective-permute-done.22.refs_6_) | copy-start | bytes 2457604
  134.1 24.3 %collective-permute-start.26 = (bf16[320,1280]{1,0:T(8,128)(2,1)}, bf16[320,1280]{1,0:T(8,128)(2,1)}, u32[]{:S(2)}, u32[]{:S(2)}) collective-permute-start(bf16[320,1280]{1,0:T(8,128)(2,1)} %broadcast_select_fusion.1), channel_id=1, source_target_pairs={{0,2},{1,5},{2,0},{3,7},{4,6},{5,1},{6,4},{7,3},{8,10},{9,13},{10,... | collective-permute-start | bytes 2457608 | tf_op jit(solution)/shard_map/ppermute | solution.py:68
  136.9 30.9 %all-to-all-start.2 = ((bf16[16,80,320]{2,1,0:T(8,128)(2,1)}), bf16[16,80,320]{2,1,0:T(8,128)(2,1)}, u32[]{:S(2)}, u32[]{:S(2)}) async-start(bf16[16,80,320]{2,1,0:T(8,128)(2,1)} %bitcast.67), calls=%async_computation.2 | async-start | bytes 1966080 | tf_op jit(solution)/shard_map/all_to_all | solution.py:487
  141.2 24.4 %collective-permute-start.14 = (bf16[64,5120]{1,0:T(8,128)(2,1)}, bf16[64,5120]{1,0:T(8,128)(2,1)}, u32[]{:S(2)}, u32[]{:S(2)}) collective-permute-start(bf16[64,5120]{1,0:T(8,128)(2,1)} %attend_slots.1.refs_0_), channel_id=1, source_target_pairs={{0,12},{4,8},{8,4},{12,0},{16,28},{20,24},{24,20},{28,16},{32,44},... | collective-permute-start | bytes 1966088 | tf_op jit(solution)/shard_map/ppermute | solution.py:44
  157.8 16.2 %collective-permute-start.17 = (bf16[64,5120]{1,0:T(8,128)(2,1)}, bf16[64,5120]{1,0:T(8,128)(2,1)}, u32[]{:S(2)}, u32[]{:S(2)}) collective-permute-start(bf16[64,5120]{1,0:T(8,128)(2,1)} %broadcast_select_fusion.2), channel_id=1, source_target_pairs={{0,16},{1,49},{2,18},{3,51},{4,20},{5,53},{6,22},{7,55},{8,24},{9,... | collective-permute-start | bytes 1966088 | tf_op jit(solution)/shard_map/ppermute | solution.py:68
  157.9 25.4 %collective-permute-start.21 = (bf16[320,1280]{1,0:T(8,128)(2,1)S(1)}, bf16[320,1280]{1,0:T(8,128)(2,1)}, u32[]{:S(2)}, u32[]{:S(2)}) collective-permute-start(bf16[320,1280]{1,0:T(8,128)(2,1)S(1)} %bitcast.64), channel_id=1, source_target_pairs={{0,1},{1,0},{2,3},{3,2},{4,5},{5,4},{6,7},{7,6},{8,9},{9,8},{10,11... | collective-permute-start | bytes 2457608 | tf_op jit(solution)/shard_map/ppermute | solution.py:57
  157.9 26.9 %collective-permute-start.23 = (bf16[320,1280]{1,0:T(8,128)(2,1)S(1)}, bf16[320,1280]{1,0:T(8,128)(2,1)}, u32[]{:S(2)}, u32[]{:S(2)}) collective-permute-start(bf16[320,1280]{1,0:T(8,128)(2,1)S(1)} %collective-permute-done.22.refs_6_), channel_id=1, source_target_pairs={{0,1},{1,0},{2,3},{3,2},{4,5},{5,4},{6,7},{7,6},{8,9},{9,8},{10,11... | collective-permute-start | bytes 2457608 | tf_op jit(solution)/shard_map/ppermute | solution.py:57
  158.4 28.1 %collective-permute-start.25 = (bf16[320,1280]{1,0:T(8,128)(2,1)}, bf16[320,1280]{1,0:T(8,128)(2,1)}, u32[]{:S(2)}, u32[]{:S(2)}) collective-permute-start(bf16[320,1280]{1,0:T(8,128)(2,1)} %collective-permute-done.24.refs_8_), channel_id=1, source_target_pairs={{0,1},{1,0},{2,3},{3,2},{4,5},{5,4},{6,7},{7,6},{8,9},{9,8},{10,11... | collective-permute-start | bytes 2457608 | tf_op jit(solution)/shard_map/ppermute | solution.py:57
  165.6 21.3 %collective-permute-start.27 = (bf16[320,1280]{1,0:T(8,128)(2,1)}, bf16[320,1280]{1,0:T(8,128)(2,1)}, u32[]{:S(2)}, u32[]{:S(2)}) collective-permute-start(bf16[320,1280]{1,0:T(8,128)(2,1)} %collective-permute-done.26.refs_10_), channel_id=1, source_target_pairs={{0,1},{1,0},{2,3},{3,2},{4,5},{5,4},{6,7},{7,6},{8,9},{9,8},{10,11... | collective-permute-start | bytes 2457608 | tf_op jit(solution)/shard_map/ppermute | solution.py:57
  174.1 30.4 %collective-permute-start.28 = (bf16[448,1280]{1,0:T(8,128)(2,1)}, bf16[448,1280]{1,0:T(8,128)(2,1)}, u32[]{:S(2)}, u32[]{:S(2)}) collective-permute-start(bf16[448,1280]{1,0:T(8,128)(2,1)} %copy.47), channel_id=1, source_target_pairs={{0,64},{1,65},{2,66},{3,67},{4,68},{5,69},{6,70},{7,71},{8,72},{9,... | collective-permute-start | bytes 3440648 | tf_op jit(solution)/shard_map/ppermute | solution.py:33
  183.2 23.7 %collective-permute-start.18 = (bf16[64,5120]{1,0:T(8,128)(2,1)}, bf16[64,5120]{1,0:T(8,128)(2,1)}, u32[]{:S(2)}, u32[]{:S(2)}) collective-permute-start(bf16[64,5120]{1,0:T(8,128)(2,1)} %collective-permute-done.14.refs_0_), channel_id=1, source_target_pairs={{0,16},{4,20},{8,24},{12,28},{16,32},{20,36},{24,40},{28,44},{32,4... | collective-permute-start | bytes 1966088 | tf_op jit(solution)/shard_map/ppermute | solution.py:39
  184.7 22.2 %collective-permute-start.19 = (bf16[64,5120]{1,0:T(8,128)(2,1)}, bf16[64,5120]{1,0:T(8,128)(2,1)}, u32[]{:S(2)}, u32[]{:S(2)}) collective-permute-start(bf16[64,5120]{1,0:T(8,128)(2,1)} %collective-permute-done.14.refs_0_), channel_id=1, source_target_pairs={{0,48},{4,52},{8,56},{12,60},{16,0},{20,4},{24,8},{28,12},{32,16},... | collective-permute-start | bytes 1966088 | tf_op jit(solution)/shard_map/ppermute | solution.py:39
  186.5 20.5 %collective-permute-start.20 = (bf16[64,5120]{1,0:T(8,128)(2,1)}, bf16[64,5120]{1,0:T(8,128)(2,1)}, u32[]{:S(2)}, u32[]{:S(2)}) collective-permute-start(bf16[64,5120]{1,0:T(8,128)(2,1)} %collective-permute-done.17.refs_3_), channel_id=1, source_target_pairs={{0,12},{4,8},{8,4},{12,0},{16,28},{20,24},{24,20},{28,16},{32,44},... | collective-permute-start | bytes 1966088 | tf_op jit(solution)/shard_map/ppermute | solution.py:44
  187.5 8.6 %copy-start.9 = (bf16[10,8,40,128]{3,1,2,0:T(8,128)(2,1)S(1)}, bf16[10,8,40,128]{3,1,2,0:T(8,128)(2,1)}, u32[]{:S(2)}) copy-start(bf16[10,8,40,128]{3,1,2,0:T(8,128)(2,1)} %copy.60) | copy-start | bytes 2457604
  198.1 21.7 %all-to-all-start.3 = ((bf16[80,16,320]{2,0,1:T(8,128)(2,1)}), bf16[80,16,320]{2,0,1:T(8,128)(2,1)S(1)}, u32[]{:S(2)}, u32[]{:S(2)}) async-start(bf16[80,16,320]{2,0,1:T(8,128)(2,1)} %copy.51), calls=%async_computation.3 | async-start | bytes 1966080 | tf_op jit(solution)/shard_map/all_to_all | solution.py:497
  219.8 14.3 %all-to-all-start.1 = ((bf16[8,64,640]{2,1,0:T(8,128)(2,1)}), bf16[8,64,640]{2,1,0:T(8,128)(2,1)S(1)}, u32[]{:S(2)}, u32[]{:S(2)}) async-start(bf16[8,64,640]{2,1,0:T(8,128)(2,1)} %product.7), calls=%async_computation.1 | async-start | bytes 1310720 | tf_op jit(solution)/shard_map/all_to_all | solution.py:131
  228.4 20.9 %collective-permute-start.29 = (bf16[1280,320]{0,1:T(8,128)(2,1)}, bf16[1280,320]{0,1:T(8,128)(2,1)}, u32[]{:S(2)}, u32[]{:S(2)}) collective-permute-start(bf16[1280,320]{0,1:T(8,128)(2,1)} %copy.52), channel_id=1, source_target_pairs={{0,64},{1,65},{2,66},{3,67},{4,68},{5,69},{6,70},{7,71},{8,72},{9,... | collective-permute-start | bytes 2457608 | tf_op jit(solution)/shard_map/ppermute | solution.py:33
  236.0 2.8 %copy-start.7 = (bf16[1,16,4,5120]{3,2,1,0:T(4,128)(2,1)S(1)}, bf16[1,16,4,5120]{3,2,1,0:T(4,128)(2,1)}, u32[]{:S(2)}) copy-start(bf16[1,16,4,5120]{3,2,1,0:T(4,128)(2,1)} %param.15) | copy-start | bytes 1966084
where the time goes:
time: 254 us; the launch traced here: 252 us
  waiting for transfers between devices  84.1 us (33%)
  starting transfers between devices  61.5 us (24%)
  Pallas kernels  48 us (19%)
  local copies, waits for them, and re-layouts  31.9 us (13%)
  other arithmetic  15.8 us (6%)
  matrix products  9.76 us (4%)
    pallas_call x4, Pallas kernels, product(): pl.pallas_call(functools.partial(product_kernel, blocks, groups, other is...  35.6 us
    ppermute x8, waiting for transfers between devices, along_z(): return lax.ppermute(value, 'shard', pairs)  21.1 us
    ppermute x2, waiting for transfers between devices, next_y(): return lax.ppermute(value, 'shard', [(s, s ^ 1) for s in range(count)])  14.6 us
    all_to_all x2, waiting for transfers between devices, to_owners(): lax.all_to_all(ordered, 'shard', split_axis=0, concat_axis=0, axis_index_...  14.3 us
    ppermute x8, starting transfers between devices, along_z(): return lax.ppermute(value, 'shard', pairs)  14.1 us
    pallas_call x1, Pallas kernels, attend_slots(): pl.pallas_call(attention_kernel, out_shape=jax.ShapeDtypeStruct((rows * S...  12.3 us
    ppermute x2, waiting for transfers between devices, other_chip(): return lax.ppermute(value, 'rep', [(r, r ^ 2) for r in range(4)])  10.5 us
    ppermute x2, starting transfers between devices, shifted(): lax.ppermute(value, axis, [(source, source + steps) for source in range(i...  10.4 us
  transfers between devices with their start and end apart: 34, of which 11 were waited for; matrix products, arithmetic and copies ran while one was open for 19% of the time, Pallas kernels for 15%

commit v1 on v0

--- a/solution.py
+++ b/solution.py
@@ -478,28 +478,30 @@
     pair_bias = lax.dynamic_slice_in_dim(bias, (shard_index ^ 1) * width, width, 1)
     same, mirror = gather_rows(slot_columns(normed, rep_index))
     order = jnp.concatenate([near, far, low_first])
-    folded_qkv = rotate_column_part(
-        after(jnp.concatenate(qkv_slots[0], axis=1), same[3]), rep_index, rep_total
-    )
-    mine = product(same + mirror, qkv_slots[0], own_bias, after(order, folded_qkv), partial=True)
+    spread = lax.all_to_all(own_out, "shard", split_axis=0, concat_axis=1, tiled=True)
+    turned = rotate_columns(after(spread, same[3]))
+    mine = product(same + mirror, qkv_slots[0], own_bias, after(order, turned), partial=True)
     part = product(same + mirror, qkv_slots[1], pair_bias, order, other=mine)
     packed = to_owners(part)
-    spread = lax.all_to_all(
-        after(own_out, part), "shard", split_axis=0, concat_axis=1, tiled=True
+    folded_qkv = rotate_column_part(
+        after(jnp.concatenate(qkv_slots[0], axis=1), part), rep_index, rep_total
     )
     out_slots = gather_weights(after(own_out.T, qkv_slots[1][2]))
+    weights = out_slots[0] + out_slots[1]
+    folded_out = lax.all_to_all(
+        after(turned, part), "shard", split_axis=1, concat_axis=0, tiled=True
+    )
+    packed = after(packed, folded_qkv, *weights)
     attended = attend_slots(packed, cache_keys[0], cache_values[0], lengths[0], rep_index)
     same, mirror = gather_rows(attended)
-    weights = out_slots[0] + out_slots[1]
     no_bias = jnp.zeros((1, own_out.shape[1]), jnp.float32)
     part = product(same, weights, no_bias, jnp.concatenate([near, low_first]))
-    turned = after(rotate_columns(after(spread, attended)), part)
-    folded_out = lax.all_to_all(turned, "shard", split_axis=1, concat_axis=0, tiled=True)
     part = product(mirror, weights, no_bias, jnp.concatenate([far, low_first]), buffer=part)
     projected = to_owners(part)
     projected = projected.transpose(1, 0, 2).reshape(rows, STEPS, D).astype(jnp.float32)
     layer_out = (states + projected).astype(jnp.bfloat16)[None]
-    sent_qkv, sent_out = shifted((folded_qkv, folded_out), "role", 1)
+    sent_qkv = shifted(folded_qkv, "role", 1)
+    sent_out = shifted(folded_out, "role", 1)
     new_qkv = jnp.where(trainer_side, folded_qkv, sent_qkv)
     new_o = jnp.where(trainer_side, folded_out, sent_out)
     return (layer_out, new_qkv.T[None], new_o[None])

time: 254 us -> 248 us (0.976)
  waiting for transfers between devices: 84.1 us -> 71.6 us
  other arithmetic: 15.8 us -> 19.5 us
    all_to_all x2, waiting for transfers between devices: 14.3 us -> 5.48 us  [to_owners(): lax.all_to_all(ordered, 'shard', split_axis=0, concat_axis=0, axis_index_...]
    ppermute x2, waiting for transfers between devices: 8.42 us -> 0.01 us  [shifted(): lax.ppermute(value, axis, [(source, source + steps) for source in range(i...]
    ppermute x4, waiting for transfers between devices: 3.54 us -> 10.1 us  [crossed(): return lax.ppermute(value, ('shard', 'rep'), pairs)]
    unnamed x37 -> x40, local copies, waits for them, and re-layouts: 7.29 us -> 13.2 us
    ppermute x2, waiting for transfers between devices: 10.5 us -> 5.44 us  [other_chip(): return lax.ppermute(value, 'rep', [(r, r ^ 2) for r in range(4)])]
    ppermute x4, waiting for transfers between devices: 7.19 us -> 2.09 us  [mirror_y(): return lax.ppermute(value, 'shard', [(s, s ^ 3) for s in range(count)])]
    ppermute x2, waiting for transfers between devices: 14.6 us -> 18.9 us  [next_y(): return lax.ppermute(value, 'shard', [(s, s ^ 1) for s in range(count)])]
    ppermute x2, starting transfers between devices: 10.4 us -> 6.66 us  [shifted(): lax.ppermute(value, axis, [(source, source + steps) for source in range(i...]
  transfers between devices with their start and end apart: 34 -> 34, of which waited for: 11 -> 11; matrix products, arithmetic and copies ran while one was open for 19% -> 21% of each run, Pallas kernels for 15% -> 15%
where the time goes in v1:
time: 248 us; the launch traced here: 245 us
  waiting for transfers between devices  71.6 us (29%)
  starting transfers between devices  60.6 us (24%)
  Pallas kernels  48 us (19%)
  local copies, waits for them, and re-layouts  33.5 us (14%)
  other arithmetic  19.5 us (8%)
  matrix products  10.6 us (4%)
    pallas_call x4, Pallas kernels, product(): pl.pallas_call(functools.partial(product_kernel, blocks, groups, other is...  35.7 us
    ppermute x8, waiting for transfers between devices, along_z(): return lax.ppermute(value, 'shard', pairs)  22.4 us
    ppermute x2, waiting for transfers between devices, next_y(): return lax.ppermute(value, 'shard', [(s, s ^ 1) for s in range(count)])  18.9 us
    ppermute x8, starting transfers between devices, along_z(): return lax.ppermute(value, 'shard', pairs)  14.2 us
    unnamed x40, local copies, waits for them, and re-layouts  13.2 us
    pallas_call x1, Pallas kernels, attend_slots(): pl.pallas_call(attention_kernel, out_shape=jax.ShapeDtypeStruct((rows * S...  12.3 us
    ppermute x4, starting transfers between devices, mirror_y(): return lax.ppermute(value, 'shard', [(s, s ^ 3) for s in range(count)])  10.8 us
    all_to_all x2, starting transfers between devices, to_owners(): lax.all_to_all(ordered, 'shard', split_axis=0, concat_axis=0, axis_index_...  10.4 us
  transfers between devices with their start and end apart: 34, of which 11 were waited for; matrix products, arithmetic and copies ran while one was open for 21% of the time, Pallas kernels for 15%

profile of v1, /device:TPU:0, one launch (start us, length us, event | category | flops | bytes accessed | tf_op | source)
XLA Modules:
  0.0 245.1 jit_solution(12709735258084034160)
XLA Ops:
  0.7 1.5 reshape.172
  3.1 2.1 collective-permute-start
  5.2 2.2 collective-permute-start.1
  7.4 3.0 %collective-permute-start.3 = (bf16[64,5120]{1,0:T(8,128)(2,1)S(1)}, bf16[64,5120]{1,0:T(8,128)(2,1)}, u32[]{:S(2)}, u32[]{:S(2)}) collective-permute-start(bf16[64,5120]{1,0:T(8,128)(2,1)S(1)} %pad_maximum_fusion.1.refs_0_), channel_id=1, source_target_pairs={{0,12},{4,8},{8,4},{12,0},{16,28},{20,24},{24,20},{28,16},{32,44},... | collective-permute-start | bytes 1966088 | tf_op jit(solution)/shard_map/ppermute | solution.py:44
  10.4 1.5 collective-permute-start.9
  11.9 1.3 copy.45
  13.3 4.5 %all-to-all-start = ((bf16[16,80,320]{2,1,0:T(8,128)(2,1)}), bf16[16,80,320]{2,1,0:T(8,128)(2,1)}, u32[]{:S(2)}, u32[]{:S(2)}) async-start(bf16[16,80,320]{2,1,0:T(8,128)(2,1)} %bitcast.66), calls=%async_computation | async-start | bytes 1966080 | tf_op jit(solution)/shard_map/all_to_all | solution.py:481
  18.2 4.0 %collective-permute-done.refs_1_ = bf16[64,5120]{1,0:T(8,128)(2,1)} collective-permute-done((bf16[64,5120]{1,0:T(8,128)(2,1)S(1)}, bf16[64,5120]{1,0:T(8,128)(2,1)}, u32[]{:S(2)}, u32[]{:S(2)}) %collective-permute-start) | collective-permute-done | bytes 655392 | tf_op jit(solution)/shard_map/ppermute | solution.py:39
  22.2 1.7 collective-permute-start.7
  23.9 5.8 %collective-permute-done.1.refs_2_ = bf16[64,5120]{1,0:T(8,128)(2,1)} collective-permute-done((bf16[64,5120]{1,0:T(8,128)(2,1)S(1)}, bf16[64,5120]{1,0:T(8,128)(2,1)}, u32[]{:S(2)}, u32[]{:S(2)}) %collective-permute-start.1) | collective-permute-done | bytes 655392 | tf_op jit(solution)/shard_map/ppermute | solution.py:39
  29.6 2.0 broadcast_select_fusion.3
  31.6 5.4 %collective-permute-done.9.refs_10_ = bf16[448,1280]{1,0:T(8,128)(2,1)S(1)} collective-permute-done((bf16[448,1280]{1,0:T(8,128)(2,1)}, bf16[448,1280]{1,0:T(8,128)(2,1)S(1)}, u32[]{:S(2)}, u32[]{:S(2)}) %collective-permute-start.9) | collective-permute-done | bytes 1146912 | tf_op jit(solution)/shard_map/ppermute | solution.py:53
  37.1 18.9 %collective-permute-done.7.refs_8_ = bf16[448,1280]{1,0:T(8,128)(2,1)} collective-permute-done((bf16[448,1280]{1,0:T(8,128)(2,1)}, bf16[448,1280]{1,0:T(8,128)(2,1)}, u32[]{:S(2)}, u32[]{:S(2)}) %collective-permute-start.7) | collective-permute-done | bytes 1146912 | tf_op jit(solution)/shard_map/ppermute | solution.py:49
  56.0 2.4 broadcast_select_fusion
  60.2 1.5 collective-permute-start.4
  62.6 1.8 collective-permute-start.5
  64.4 10.1 %collective-permute-done.10.refs_10_ = bf16[448,1280]{1,0:T(8,128)(2,1)} collective-permute-done((bf16[448,1280]{1,0:T(8,128)(2,1)}, bf16[448,1280]{1,0:T(8,128)(2,1)}, u32[]{:S(2)}, u32[]{:S(2)}) %collective-permute-start.10) | collective-permute-done | bytes 1146912 | tf_op jit(solution)/shard_map/ppermute | solution.py:68
  74.6 2.1 collective-permute-start.6
  77.2 0.8 collective-permute-start.17
  78.7 2.4 copy.46
  81.1 2.6 %all_to_all.37 = bf16[80,5120]{1,0:T(8,128)(2,1)} reshape(bf16[80,16,320]{2,1,0:T(8,128)(2,1)} %copy.46) | data formatting | bytes 1638400 | tf_op jit(solution)/shard_map/all_to_all | solution.py:481
  83.7 1.3 copy.56
  85.6 1.5 multiply_convert_fusion.1
  87.1 1.0 copy.60
  88.2 2.1 collective-permute-done.6.refs_7_
  90.8 8.9 %product.4.refs_13_ = bf16[512,448]{1,0:T(8,128)(2,1)} custom-call(s32[9]{0:T(128)} %pad_add_fusion.1.order_ref, bf16[64,5120]{1,0:T(8,128)(2,1)} %copy-done.4, bf16[64,5120]{1,0:T(8,128)(2,1)} %collective-permute-done.refs_1_, bf16[64,5120]{1,0:T(8,128)(2,1)} %collective-permute-done.1.refs_2_, bf16[64,5120]{1,0:T(8,128)(2,1)} %collective-permute-done.2.refs_3_, ...), custom_call_target="tpu_custom_call" | custom-call | flops 2348810240 | bytes 9830400 | tf_op jit(solution)/shard_map/product/pallas_call | solution.py:434
  99.7 2.5 %broadcast_select_fusion.1 = bf16[320,1280]{1,0:T(8,128)(2,1)} fusion(bf16[320,1280]{1,0:T(8,128)(2,1)} %collective-permute-done.17.refs_8_, bf16[320,1280]{1,0:T(8,128)(2,1)S(1)} %collective-permute-done.15.refs_6_, pred[]{:T(512)S(6)} %eq.59), kind=kLoop, calls=%fused_computation.12 | loop fusion | flops 409600 | bytes 2457601 | tf_op jit(solution)/shard_map/jit(_where)/select_n | solution.py:61
  102.7 3.8 %pad_maximum_fusion = bf16[448,5120]{1,0:T(8,128)(2,1)} fusion(bf16[448,1280]{1,0:T(8,128)(2,1)} %collective-permute-done.13.refs_11_, bf16[448,1280]{1,0:T(8,128)(2,1)S(1)} %copy-done.1, bf16[448,1280]{1,0:T(8,128)(2,1)} %collective-permute-done.12.refs_9_, bf16[448,1280]{1,0:T(8,128)(2,1)} %bitcast.5.refs_8_), kind=kLoop, calls=%fused_computation | loop fusion | flops 18350080 | bytes 9175040 | tf_op jit(solution)/shard_map/concatenate | solution.py:487
  107.0 1.0 copy-done.10
  108.0 9.6 %product.5 = bf16[8,64,896]{2,1,0:T(8,128)(2,1)} custom-call(s32[9]{0:T(128)} %pad_add_fusion.1.order_ref, bf16[64,5120]{1,0:T(8,128)(2,1)} %copy-done.4, bf16[64,5120]{1,0:T(8,128)(2,1)} %collective-permute-done.refs_1_, bf16[64,5120]{1,0:T(8,128)(2,1)} %collective-permute-done.1.refs_2_, bf16[64,5120]{1,0:T(8,128)(2,1)} %collective-permute-done.2.refs_3_, ...), custom_call_target="tpu_custom_call" | custom-call | flops 2348810240 | bytes 9830400 | tf_op jit(solution)/shard_map/product/pallas_call | solution.py:434
  117.7 5.3 %all-to-all-start.1 = ((bf16[8,64,896]{2,1,0:T(8,128)(2,1)}), bf16[8,64,896]{2,1,0:T(8,128)(2,1)}, u32[]{:S(2)}, u32[]{:S(2)}) async-start(bf16[8,64,896]{2,1,0:T(8,128)(2,1)} %product.5), calls=%async_computation.1 | async-start | bytes 1835008 | tf_op jit(solution)/shard_map/all_to_all | solution.py:131
  123.0 3.5 %copy.58 = bf16[56,8,40,128]{3,2,1,0:T(8,128)(2,1)S(1)} copy(bf16[56,8,40,128]{3,1,2,0:T(8,128)(2,1)} %bitcast.55) | data formatting | bytes 9175040
  126.6 2.6 %fusion.7 = f32[448,40,128]{2,1,0:T(8,128)S(1)} fusion(bf16[448,40,128]{2,1,0:T(8,128)(2,1)S(1)} %bitcast.56), kind=kOutput, calls=%fused_computation.30 | convolution fusion | flops 587792384 | bytes 13762560 | tf_op jit(solution)/shard_map/mab,by->may/dot_general | solution.py:165
  129.2 5.9 %fusion = bf16[448,10,128]{2,1,0:T(8,128)(2,1)} fusion(f32[448,40,128]{2,1,0:T(8,128)S(1)} %fusion.7, f32[10,10]{0,1:T(8,128)S(1)} %get-tuple-element.42, f32[10,10]{0,1:T(8,128)S(1)} %get-tuple-element.40, f32[10,10]{0,1:T(8,128)S(1)} %get-tuple-element.41, f32[10,10]{0,1:T(8,128)S(1)} %get-tuple-element.39), kind=kOutput, calls=%fused_computation.3 | convolution fusion | flops 276399296 | bytes 10323520 | tf_op jit(solution)/shard_map/may,ax->mxy/dot_general | solution.py:177
  135.1 3.1 %copy.47 = bf16[448,10,128]{0,2,1:T(8,128)(2,1)S(1)} copy(bf16[448,10,128]{2,1,0:T(8,128)(2,1)} %fusion) | data formatting | bytes 2293760 | tf_op jit(solution)/shard_map/convert_element_type | solution.py:178
  138.9 12.3 %attend_slots.1.refs_0_ = bf16[64,5120]{1,0:T(8,128)(2,1)} custom-call(s32[1]{0:T(128)} %bitcast.1.part_ref, s32[16]{0:T(128)} %bitcast.72, bf16[8,64,896]{2,1,0:T(8,128)(2,1)} %all-to-all-done.1.packed_ref, f32[64,128]{1,0:T(8,128)} %get-tuple-element.46.cosine_ref, f32[64,128]{1,0:T(8,128)} %get-tuple-element.47.sine_ref, bf16[16,128,1024]{2,1,0:T(8,128)(2,1)} %bitcast.64, ...), custom_call_target="tpu_custom_call" | custom-call | flops 2000000000 | bytes 10000000 | tf_op jit(solution)/shard_map/attend_slots/pallas_call | solution.py:312
  151.3 1.4 collective-permute-start.22
  152.6 1.9 collective-permute-start.23
  154.5 2.6 %collective-permute-start.21 = (bf16[64,5120]{1,0:T(8,128)(2,1)}, bf16[64,5120]{1,0:T(8,128)(2,1)}, u32[]{:S(2)}, u32[]{:S(2)}) collective-permute-start(bf16[64,5120]{1,0:T(8,128)(2,1)} %attend_slots.1.refs_0_), channel_id=1, source_target_pairs={{0,12},{4,8},{8,4},{12,0},{16,28},{20,24},{24,20},{28,16},{32,44},... | collective-permute-start | bytes 1966088 | tf_op jit(solution)/shard_map/ppermute | solution.py:44
  157.1 12.4 %collective-permute-done.22.refs_1_ = bf16[64,5120]{1,0:T(8,128)(2,1)S(1)} collective-permute-done((bf16[64,5120]{1,0:T(8,128)(2,1)}, bf16[64,5120]{1,0:T(8,128)(2,1)S(1)}, u32[]{:S(2)}, u32[]{:S(2)}) %collective-permute-start.22) | collective-permute-done | bytes 655392 | tf_op jit(solution)/shard_map/ppermute | solution.py:39
  170.3 1.0 broadcast_select_fusion.2
  171.4 0.9 collective-permute-start.24
  172.2 1.4 copy.49
  173.7 5.3 %collective-permute-start.28 = (bf16[448,1280]{1,0:T(8,128)(2,1)}, bf16[448,1280]{1,0:T(8,128)(2,1)}, u32[]{:S(2)}, u32[]{:S(2)}) collective-permute-start(bf16[448,1280]{1,0:T(8,128)(2,1)} %copy.49), channel_id=1, source_target_pairs={{0,64},{1,65},{2,66},{3,67},{4,68},{5,69},{6,70},{7,71},{8,72},{9,... | collective-permute-start | bytes 3440648 | tf_op jit(solution)/shard_map/ppermute | solution.py:33
  179.0 0.8 all_to_all.40
  179.8 1.2 copy.51
  180.9 6.5 %all-to-all-start.3 = ((bf16[80,16,320]{2,0,1:T(8,128)(2,1)}), bf16[80,16,320]{2,0,1:T(8,128)(2,1)S(1)}, u32[]{:S(2)}, u32[]{:S(2)}) async-start(bf16[80,16,320]{2,0,1:T(8,128)(2,1)} %copy.51), calls=%async_computation.3 | async-start | bytes 1966080 | tf_op jit(solution)/shard_map/all_to_all | solution.py:491
  187.4 2.0 collective-permute-start.25
  189.4 1.3 collective-permute-start.26
  190.7 3.1 %collective-permute-start.27 = (bf16[64,5120]{1,0:T(8,128)(2,1)}, bf16[64,5120]{1,0:T(8,128)(2,1)}, u32[]{:S(2)}, u32[]{:S(2)}) collective-permute-start(bf16[64,5120]{1,0:T(8,128)(2,1)} %collective-permute-done.24.refs_3_), channel_id=1, source_target_pairs={{0,12},{4,8},{8,4},{12,0},{16,28},{20,24},{24,20},{28,16},{32,44},... | collective-permute-start | bytes 1966088 | tf_op jit(solution)/shard_map/ppermute | solution.py:44
  195.2 7.1 %all-to-all-done.3 = bf16[80,16,320]{2,0,1:T(8,128)(2,1)S(1)} async-done(((bf16[80,16,320]{2,0,1:T(8,128)(2,1)}), bf16[80,16,320]{2,0,1:T(8,128)(2,1)S(1)}, u32[]{:S(2)}, u32[]{:S(2)}) %all-to-all-start.3) | async-done | bytes 819232 | tf_op jit(solution)/shard_map/all_to_all | solution.py:491
  202.3 1.3 copy.52
  203.6 1.3 collective-permute-start.29
  204.9 2.5 %copy.50 = bf16[448,1280]{0,1:T(8,128)(2,1)} copy(bf16[448,1280]{1,0:T(8,128)(2,1)} %collective-permute-done.28) | data formatting | bytes 2293760 | tf_op jit(solution)/shard_map/ppermute | solution.py:33
  208.0 8.6 %product.6.refs_13_ = bf16[8,64,640]{2,1,0:T(8,128)(2,1)} custom-call(s32[5]{0:T(128)} %pad_add_fusion.2.order_ref, bf16[64,5120]{1,0:T(8,128)(2,1)} %attend_slots.1.refs_0_, bf16[64,5120]{1,0:T(8,128)(2,1)} %copy-done.8, bf16[64,5120]{1,0:T(8,128)(2,1)} %copy-done.9, bf16[64,5120]{1,0:T(8,128)(2,1)} %collective-permute-done.24.refs_3_, ...), custom_call_target="tpu_custom_call" | custom-call | flops 1677721600 | bytes 9175040 | tf_op jit(solution)/shard_map/product/pallas_call | solution.py:434
  216.6 8.6 %product.7 = bf16[8,64,640]{2,1,0:T(8,128)(2,1)} custom-call(s32[5]{0:T(128)} %pad_add_fusion.order_ref, bf16[64,5120]{1,0:T(8,128)(2,1)} %collective-permute-done.21.refs_0_, bf16[64,5120]{1,0:T(8,128)(2,1)} %collective-permute-done.25.refs_1_, bf16[64,5120]{1,0:T(8,128)(2,1)} %collective-permute-done.26.refs_2_, ...), custom_call_target="tpu_custom_call", output_to_operand_aliasing={{}: (14, {})} | custom-call | flops 1677721600 | bytes 9175040 | tf_op jit(solution)/shard_map/product/pallas_call | solution.py:434
  225.1 5.1 %all-to-all-start.2 = ((bf16[8,64,640]{2,1,0:T(8,128)(2,1)}), bf16[8,64,640]{2,1,0:T(8,128)(2,1)}, u32[]{:S(2)}, u32[]{:S(2)}) async-start(bf16[8,64,640]{2,1,0:T(8,128)(2,1)} %product.7), calls=%async_computation.2 | async-start | bytes 1310720 | tf_op jit(solution)/shard_map/all_to_all | solution.py:131
  230.2 1.3 select_bitcast_fusion
  231.5 2.4 copy.54
  234.8 1.3 copy.55
  236.1 4.8 %all-to-all-done.2 = bf16[8,64,640]{2,1,0:T(8,128)(2,1)} async-done(((bf16[8,64,640]{2,1,0:T(8,128)(2,1)}), bf16[8,64,640]{2,1,0:T(8,128)(2,1)}, u32[]{:S(2)}, u32[]{:S(2)}) %all-to-all-start.2) | async-done | bytes 655392 | tf_op jit(solution)/shard_map/all_to_all | solution.py:131
  240.9 1.2 convert_bitcast_fusion
  242.1 0.8 copy.48
  244.0 1.2 add_convert_fusion
  (104 shorter events, 12.8 us)
Async XLA Ops:
  0.6 1.5 copy-start.5
  0.7 2.0 copy-start.12
  3.0 9.0 %copy-start.2 = (bf16[1,1280,320]{1,2,0:T(8,128)(2,1)S(1)}, bf16[1,1280,320]{1,2,0:T(8,128)(2,1)}, u32[]{:S(2)}) copy-start(bf16[1,1280,320]{1,2,0:T(8,128)(2,1)} %param.13) | copy-start | bytes 2457604
  3.1 10.2 %copy-start.4 = (bf16[64,5120]{1,0:T(8,128)(2,1)}, bf16[64,5120]{1,0:T(8,128)(2,1)S(1)}, u32[]{:S(2)}) copy-start(bf16[64,5120]{1,0:T(8,128)(2,1)S(1)} %pad_maximum_fusion.1.refs_0_) | copy-start | bytes 1966084
  3.1 19.1 %collective-permute-start = (bf16[64,5120]{1,0:T(8,128)(2,1)S(1)}, bf16[64,5120]{1,0:T(8,128)(2,1)}, u32[]{:S(2)}, u32[]{:S(2)}) collective-permute-start(bf16[64,5120]{1,0:T(8,128)(2,1)S(1)} %pad_maximum_fusion.1.refs_0_), channel_id=1, source_target_pairs={{0,16},{4,20},{8,24},{12,28},{16,32},{20,36},{24,40},{28,44},{32,4... | collective-permute-start | bytes 1966088 | tf_op jit(solution)/shard_map/ppermute | solution.py:39
  5.2 24.4 %collective-permute-start.1 = (bf16[64,5120]{1,0:T(8,128)(2,1)S(1)}, bf16[64,5120]{1,0:T(8,128)(2,1)}, u32[]{:S(2)}, u32[]{:S(2)}) collective-permute-start(bf16[64,5120]{1,0:T(8,128)(2,1)S(1)} %pad_maximum_fusion.1.refs_0_), channel_id=1, source_target_pairs={{0,48},{4,52},{8,56},{12,60},{16,0},{20,4},{24,8},{28,12},{32,16},... | collective-permute-start | bytes 1966088 | tf_op jit(solution)/shard_map/ppermute | solution.py:39
  7.4 52.8 %collective-permute-start.3 = (bf16[64,5120]{1,0:T(8,128)(2,1)S(1)}, bf16[64,5120]{1,0:T(8,128)(2,1)}, u32[]{:S(2)}, u32[]{:S(2)}) collective-permute-start(bf16[64,5120]{1,0:T(8,128)(2,1)S(1)} %pad_maximum_fusion.1.refs_0_), channel_id=1, source_target_pairs={{0,12},{4,8},{8,4},{12,0},{16,28},{20,24},{24,20},{28,16},{32,44},... | collective-permute-start | bytes 1966088 | tf_op jit(solution)/shard_map/ppermute | solution.py:44
  10.4 26.7 %collective-permute-start.9 = (bf16[448,1280]{1,0:T(8,128)(2,1)}, bf16[448,1280]{1,0:T(8,128)(2,1)S(1)}, u32[]{:S(2)}, u32[]{:S(2)}) collective-permute-start(bf16[448,1280]{1,0:T(8,128)(2,1)} %bitcast.5.refs_8_), channel_id=1, source_target_pairs={{0,2},{1,3},{2,0},{3,1},{4,6},{5,7},{6,4},{7,5},{8,10},{9,11},{10,... | collective-permute-start | bytes 3440648 | tf_op jit(solution)/shard_map/ppermute | solution.py:53
  11.9 64.8 %collective-permute-start.12 = (bf16[448,1280]{1,0:T(8,128)(2,1)}, bf16[448,1280]{1,0:T(8,128)(2,1)}, u32[]{:S(2)}, u32[]{:S(2)}) collective-permute-start(bf16[448,1280]{1,0:T(8,128)(2,1)} %bitcast.5.refs_8_), channel_id=1, source_target_pairs={{0,1},{1,0},{2,3},{3,2},{4,5},{5,4},{6,7},{7,6},{8,9},{9,8},{10,11... | collective-permute-start | bytes 3440648 | tf_op jit(solution)/shard_map/ppermute | solution.py:57
  13.2 4.7 %copy-start.16 = (f32[1,20]{1,0:T(1,128)S(1)}, f32[1,20]{1,0:T(1,128)}, u32[]{:S(2)}) copy-start(f32[1,20]{1,0:T(1,128)} %constant.197.clone.1) | copy-start | bytes 244
  13.2 4.8 %copy-start.14 = (f32[2,2]{0,1:T(2,128)S(1)}, f32[2,2]{0,1:T(2,128)}, u32[]{:S(2)}) copy-start(f32[2,2]{0,1:T(2,128)} %constant.214.clone) | copy-start | bytes 52
  13.3 65.5 %all-to-all-start = ((bf16[16,80,320]{2,1,0:T(8,128)(2,1)}), bf16[16,80,320]{2,1,0:T(8,128)(2,1)}, u32[]{:S(2)}, u32[]{:S(2)}) async-start(bf16[16,80,320]{2,1,0:T(8,128)(2,1)} %bitcast.66), calls=%async_computation | async-start | bytes 1966080 | tf_op jit(solution)/shard_map/all_to_all | solution.py:481
  22.2 33.8 %collective-permute-start.7 = (bf16[448,1280]{1,0:T(8,128)(2,1)}, bf16[448,1280]{1,0:T(8,128)(2,1)}, u32[]{:S(2)}, u32[]{:S(2)}) collective-permute-start(bf16[448,1280]{1,0:T(8,128)(2,1)} %bitcast.5.refs_8_), channel_id=1, source_target_pairs={{0,4},{4,0},{8,12},{12,8},{16,20},{20,16},{24,28},{28,24},{32,36},... | collective-permute-start | bytes 3440648 | tf_op jit(solution)/shard_map/ppermute | solution.py:49
  31.6 27.3 %copy-start.13 = (s32[1,16]{1,0:T(1,128)S(1)}, s32[1,16]{1,0:T(1,128)}, u32[]{:S(2)}) copy-start(s32[1,16]{1,0:T(1,128)} %param.18) | copy-start | bytes 196
  31.6 27.4 %copy-start.11 = (bf16[1,7168]{1,0:T(2,128)(2,1)S(1)}, bf16[1,7168]{1,0:T(2,128)(2,1)}, u32[]{:S(2)}) copy-start(bf16[1,7168]{1,0:T(2,128)(2,1)} %param.12) | copy-start | bytes 43012
  31.6 31.0 %copy-start.15 = (s32[4]{0:T(128)S(1)}, s32[4]{0:T(128)}, u32[]{:S(2)}) copy-start(s32[4]{0:T(128)} %constant.213.clone) | copy-start | bytes 52
  31.6 28.6 %collective-permute-start.2 = (bf16[64,5120]{1,0:T(8,128)(2,1)}, bf16[64,5120]{1,0:T(8,128)(2,1)}, u32[]{:S(2)}, u32[]{:S(2)}) collective-permute-start(bf16[64,5120]{1,0:T(8,128)(2,1)} %broadcast_select_fusion.3), channel_id=1, source_target_pairs={{0,16},{1,49},{2,18},{3,51},{4,20},{5,53},{6,22},{7,55},{8,24},{9,... | collective-permute-start | bytes 1966088 | tf_op jit(solution)/shard_map/ppermute | solution.py:68
  37.1 24.7 %copy-start = (bf16[448,1280]{1,0:T(8,128)(2,1)}, bf16[448,1280]{1,0:T(8,128)(2,1)S(1)}, u32[]{:S(2)}) copy-start(bf16[448,1280]{1,0:T(8,128)(2,1)S(1)} %collective-permute-done.9.refs_10_) | copy-start | bytes 3440644
  58.4 16.2 %collective-permute-start.10 = (bf16[448,1280]{1,0:T(8,128)(2,1)}, bf16[448,1280]{1,0:T(8,128)(2,1)}, u32[]{:S(2)}, u32[]{:S(2)}) collective-permute-start(bf16[448,1280]{1,0:T(8,128)(2,1)} %broadcast_select_fusion), channel_id=1, source_target_pairs={{0,2},{1,5},{2,0},{3,7},{4,6},{5,1},{6,4},{7,3},{8,10},{9,13},{10,... | collective-permute-start | bytes 3440648 | tf_op jit(solution)/shard_map/ppermute | solution.py:68
  60.2 17.0 %collective-permute-start.4 = (bf16[64,5120]{1,0:T(8,128)(2,1)}, bf16[64,5120]{1,0:T(8,128)(2,1)}, u32[]{:S(2)}, u32[]{:S(2)}) collective-permute-start(bf16[64,5120]{1,0:T(8,128)(2,1)} %collective-permute-done.3.refs_4_), channel_id=1, source_target_pairs={{0,16},{4,20},{8,24},{12,28},{16,32},{20,36},{24,40},{28,44},{32,4... | collective-permute-start | bytes 1966088 | tf_op jit(solution)/shard_map/ppermute | solution.py:39
  61.8 28.5 %collective-permute-start.13 = (bf16[448,1280]{1,0:T(8,128)(2,1)S(1)}, bf16[448,1280]{1,0:T(8,128)(2,1)}, u32[]{:S(2)}, u32[]{:S(2)}) collective-permute-start(bf16[448,1280]{1,0:T(8,128)(2,1)S(1)} %collective-permute-done.9.refs_10_), channel_id=1, source_target_pairs={{0,1},{1,0},{2,3},{3,2},{4,5},{5,4},{6,7},{7,6},{8,9},{9,8},{10,11... | collective-permute-start | bytes 3440648 | tf_op jit(solution)/shard_map/ppermute | solution.py:57
  62.6 25.6 %collective-permute-start.5 = (bf16[64,5120]{1,0:T(8,128)(2,1)}, bf16[64,5120]{1,0:T(8,128)(2,1)}, u32[]{:S(2)}, u32[]{:S(2)}) collective-permute-start(bf16[64,5120]{1,0:T(8,128)(2,1)} %collective-permute-done.3.refs_4_), channel_id=1, source_target_pairs={{0,48},{4,52},{8,56},{12,60},{16,0},{20,4},{24,8},{28,12},{32,16},... | collective-permute-start | bytes 1966088 | tf_op jit(solution)/shard_map/ppermute | solution.py:39
  74.6 15.7 %collective-permute-start.6 = (bf16[64,5120]{1,0:T(8,128)(2,1)}, bf16[64,5120]{1,0:T(8,128)(2,1)}, u32[]{:S(2)}, u32[]{:S(2)}) collective-permute-start(bf16[64,5120]{1,0:T(8,128)(2,1)} %collective-permute-done.2.refs_3_), channel_id=1, source_target_pairs={{0,12},{4,8},{8,4},{12,0},{16,28},{20,24},{24,20},{28,16},{32,44},... | collective-permute-start | bytes 1966088 | tf_op jit(solution)/shard_map/ppermute | solution.py:44
  76.7 23.0 %collective-permute-start.15 = (bf16[320,1280]{1,0:T(8,128)(2,1)S(1)}, bf16[320,1280]{1,0:T(8,128)(2,1)S(1)}, u32[]{:S(2)}, u32[]{:S(2)}) collective-permute-start(bf16[320,1280]{1,0:T(8,128)(2,1)S(1)} %bitcast.61), channel_id=1, source_target_pairs={{0,2},{1,3},{2,0},{3,1},{4,6},{5,7},{6,4},{7,5},{8,10},{9,11},{10,... | collective-permute-start | bytes 2457608 | tf_op jit(solution)/shard_map/ppermute | solution.py:53
  77.2 22.5 %collective-permute-start.17 = (bf16[320,1280]{1,0:T(8,128)(2,1)S(1)}, bf16[320,1280]{1,0:T(8,128)(2,1)}, u32[]{:S(2)}, u32[]{:S(2)}) collective-permute-start(bf16[320,1280]{1,0:T(8,128)(2,1)S(1)} %bitcast.62), channel_id=1, source_target_pairs={{0,4},{4,0},{8,12},{12,8},{16,20},{20,16},{24,28},{28,24},{32,36},... | collective-permute-start | bytes 2457608 | tf_op jit(solution)/shard_map/ppermute | solution.py:49
  88.2 18.3 %collective-permute-start.8 = (bf16[448,1280]{1,0:T(8,128)(2,1)}, bf16[448,1280]{1,0:T(8,128)(2,1)}, u32[]{:S(2)}, u32[]{:S(2)}) collective-permute-start(bf16[448,1280]{1,0:T(8,128)(2,1)} %collective-permute-done.7.refs_8_), channel_id=1, source_target_pairs={{0,1},{1,0},{2,3},{3,2},{4,5},{5,4},{6,7},{7,6},{8,9},{9,8},{10,11... | collective-permute-start | bytes 3440648 | tf_op jit(solution)/shard_map/ppermute | solution.py:57
  90.3 47.9 %collective-permute-start.14 = (bf16[320,1280]{1,0:T(8,128)(2,1)S(1)}, bf16[320,1280]{1,0:T(8,128)(2,1)}, u32[]{:S(2)}, u32[]{:S(2)}) collective-permute-start(bf16[320,1280]{1,0:T(8,128)(2,1)S(1)} %bitcast.63), channel_id=1, source_target_pairs={{0,1},{1,0},{2,3},{3,2},{4,5},{5,4},{6,7},{7,6},{8,9},{9,8},{10,11... | collective-permute-start | bytes 2457608 | tf_op jit(solution)/shard_map/ppermute | solution.py:57
  90.3 16.8 %collective-permute-start.11 = (bf16[448,1280]{1,0:T(8,128)(2,1)}, bf16[448,1280]{1,0:T(8,128)(2,1)S(1)}, u32[]{:S(2)}, u32[]{:S(2)}) collective-permute-start(bf16[448,1280]{1,0:T(8,128)(2,1)} %collective-permute-done.10.refs_10_), channel_id=1, source_target_pairs={{0,1},{1,0},{2,3},{3,2},{4,5},{5,4},{6,7},{7,6},{8,9},{9,8},{10,11... | collective-permute-start | bytes 3440648 | tf_op jit(solution)/shard_map/ppermute | solution.py:57
  99.7 3.1 %copy-start.1 = (bf16[448,1280]{1,0:T(8,128)(2,1)S(1)}, bf16[448,1280]{1,0:T(8,128)(2,1)}, u32[]{:S(2)}) copy-start(bf16[448,1280]{1,0:T(8,128)(2,1)} %copy-done) | copy-start | bytes 3440644
  99.7 6.8 %copy-start.3 = (bf16[320,1280]{1,0:T(8,128)(2,1)}, bf16[320,1280]{1,0:T(8,128)(2,1)S(1)}, u32[]{:S(2)}) copy-start(bf16[320,1280]{1,0:T(8,128)(2,1)S(1)} %collective-permute-done.15.refs_6_) | copy-start | bytes 2457604
  102.2 24.3 %collective-permute-start.19 = (bf16[320,1280]{1,0:T(8,128)(2,1)}, bf16[320,1280]{1,0:T(8,128)(2,1)}, u32[]{:S(2)}, u32[]{:S(2)}) collective-permute-start(bf16[320,1280]{1,0:T(8,128)(2,1)} %broadcast_select_fusion.1), channel_id=1, source_target_pairs={{0,2},{1,5},{2,0},{3,7},{4,6},{5,1},{6,4},{7,3},{8,10},{9,13},{10,... | collective-permute-start | bytes 2457608 | tf_op jit(solution)/shard_map/ppermute | solution.py:68
  106.5 31.7 %collective-permute-start.16 = (bf16[320,1280]{1,0:T(8,128)(2,1)S(1)}, bf16[320,1280]{1,0:T(8,128)(2,1)}, u32[]{:S(2)}, u32[]{:S(2)}) collective-permute-start(bf16[320,1280]{1,0:T(8,128)(2,1)S(1)} %collective-permute-done.15.refs_6_), channel_id=1, source_target_pairs={{0,1},{1,0},{2,3},{3,2},{4,5},{5,4},{6,7},{7,6},{8,9},{9,8},{10,11... | collective-permute-start | bytes 2457608 | tf_op jit(solution)/shard_map/ppermute | solution.py:57
  106.5 31.7 %collective-permute-start.18 = (bf16[320,1280]{1,0:T(8,128)(2,1)}, bf16[320,1280]{1,0:T(8,128)(2,1)}, u32[]{:S(2)}, u32[]{:S(2)}) collective-permute-start(bf16[320,1280]{1,0:T(8,128)(2,1)} %collective-permute-done.17.refs_8_), channel_id=1, source_target_pairs={{0,1},{1,0},{2,3},{3,2},{4,5},{5,4},{6,7},{7,6},{8,9},{9,8},{10,11... | collective-permute-start | bytes 2457608 | tf_op jit(solution)/shard_map/ppermute | solution.py:57
  107.0 1.0 copy-start.10
  117.7 21.2 %all-to-all-start.1 = ((bf16[8,64,896]{2,1,0:T(8,128)(2,1)}), bf16[8,64,896]{2,1,0:T(8,128)(2,1)}, u32[]{:S(2)}, u32[]{:S(2)}) async-start(bf16[8,64,896]{2,1,0:T(8,128)(2,1)} %product.5), calls=%async_computation.1 | async-start | bytes 1835008 | tf_op jit(solution)/shard_map/all_to_all | solution.py:131
  126.5 12.4 %collective-permute-start.20 = (bf16[320,1280]{1,0:T(8,128)(2,1)}, bf16[320,1280]{1,0:T(8,128)(2,1)}, u32[]{:S(2)}, u32[]{:S(2)}) collective-permute-start(bf16[320,1280]{1,0:T(8,128)(2,1)} %collective-permute-done.19.refs_10_), channel_id=1, source_target_pairs={{0,1},{1,0},{2,3},{3,2},{4,5},{5,4},{6,7},{7,6},{8,9},{9,8},{10,11... | collective-permute-start | bytes 2457608 | tf_op jit(solution)/shard_map/ppermute | solution.py:57
  151.3 18.2 %collective-permute-start.22 = (bf16[64,5120]{1,0:T(8,128)(2,1)}, bf16[64,5120]{1,0:T(8,128)(2,1)S(1)}, u32[]{:S(2)}, u32[]{:S(2)}) collective-permute-start(bf16[64,5120]{1,0:T(8,128)(2,1)} %attend_slots.1.refs_0_), channel_id=1, source_target_pairs={{0,16},{4,20},{8,24},{12,28},{16,32},{20,36},{24,40},{28,44},{32,4... | collective-permute-start | bytes 1966088 | tf_op jit(solution)/shard_map/ppermute | solution.py:39
  152.6 17.1 %collective-permute-start.23 = (bf16[64,5120]{1,0:T(8,128)(2,1)}, bf16[64,5120]{1,0:T(8,128)(2,1)S(1)}, u32[]{:S(2)}, u32[]{:S(2)}) collective-permute-start(bf16[64,5120]{1,0:T(8,128)(2,1)} %attend_slots.1.refs_0_), channel_id=1, source_target_pairs={{0,48},{4,52},{8,56},{12,60},{16,0},{20,4},{24,8},{28,12},{32,16},... | collective-permute-start | bytes 1966088 | tf_op jit(solution)/shard_map/ppermute | solution.py:39
  154.5 32.9 %collective-permute-start.21 = (bf16[64,5120]{1,0:T(8,128)(2,1)}, bf16[64,5120]{1,0:T(8,128)(2,1)}, u32[]{:S(2)}, u32[]{:S(2)}) collective-permute-start(bf16[64,5120]{1,0:T(8,128)(2,1)} %attend_slots.1.refs_0_), channel_id=1, source_target_pairs={{0,12},{4,8},{8,4},{12,0},{16,28},{20,24},{24,20},{28,16},{32,44},... | collective-permute-start | bytes 1966088 | tf_op jit(solution)/shard_map/ppermute | solution.py:44
  169.4 0.8 copy-start.8
  170.3 1.1 copy-start.9
  171.4 7.6 %copy-start.7 = (bf16[10,8,40,128]{3,1,2,0:T(8,128)(2,1)S(1)}, bf16[10,8,40,128]{3,1,2,0:T(8,128)(2,1)}, u32[]{:S(2)}) copy-start(bf16[10,8,40,128]{3,1,2,0:T(8,128)(2,1)} %copy.60) | copy-start | bytes 2457604
  171.4 16.1 %collective-permute-start.24 = (bf16[64,5120]{1,0:T(8,128)(2,1)}, bf16[64,5120]{1,0:T(8,128)(2,1)}, u32[]{:S(2)}, u32[]{:S(2)}) collective-permute-start(bf16[64,5120]{1,0:T(8,128)(2,1)} %broadcast_select_fusion.2), channel_id=1, source_target_pairs={{0,16},{1,49},{2,18},{3,51},{4,20},{5,53},{6,22},{7,55},{8,24},{9,... | collective-permute-start | bytes 1966088 | tf_op jit(solution)/shard_map/ppermute | solution.py:68
  173.7 31.3 %collective-permute-start.28 = (bf16[448,1280]{1,0:T(8,128)(2,1)}, bf16[448,1280]{1,0:T(8,128)(2,1)}, u32[]{:S(2)}, u32[]{:S(2)}) collective-permute-start(bf16[448,1280]{1,0:T(8,128)(2,1)} %copy.49), channel_id=1, source_target_pairs={{0,64},{1,65},{2,66},{3,67},{4,68},{5,69},{6,70},{7,71},{8,72},{9,... | collective-permute-start | bytes 3440648 | tf_op jit(solution)/shard_map/ppermute | solution.py:33
  180.9 21.4 %all-to-all-start.3 = ((bf16[80,16,320]{2,0,1:T(8,128)(2,1)}), bf16[80,16,320]{2,0,1:T(8,128)(2,1)S(1)}, u32[]{:S(2)}, u32[]{:S(2)}) async-start(bf16[80,16,320]{2,0,1:T(8,128)(2,1)} %copy.51), calls=%async_computation.3 | async-start | bytes 1966080 | tf_op jit(solution)/shard_map/all_to_all | solution.py:491
  187.4 29.1 %collective-permute-start.25 = (bf16[64,5120]{1,0:T(8,128)(2,1)}, bf16[64,5120]{1,0:T(8,128)(2,1)}, u32[]{:S(2)}, u32[]{:S(2)}) collective-permute-start(bf16[64,5120]{1,0:T(8,128)(2,1)} %collective-permute-done.21.refs_0_), channel_id=1, source_target_pairs={{0,16},{4,20},{8,24},{12,28},{16,32},{20,36},{24,40},{28,44},{32,4... | collective-permute-start | bytes 1966088 | tf_op jit(solution)/shard_map/ppermute | solution.py:39
  189.4 27.1 %collective-permute-start.26 = (bf16[64,5120]{1,0:T(8,128)(2,1)}, bf16[64,5120]{1,0:T(8,128)(2,1)}, u32[]{:S(2)}, u32[]{:S(2)}) collective-permute-start(bf16[64,5120]{1,0:T(8,128)(2,1)} %collective-permute-done.21.refs_0_), channel_id=1, source_target_pairs={{0,48},{4,52},{8,56},{12,60},{16,0},{20,4},{24,8},{28,12},{32,16},... | collective-permute-start | bytes 1966088 | tf_op jit(solution)/shard_map/ppermute | solution.py:39
  190.7 25.8 %collective-permute-start.27 = (bf16[64,5120]{1,0:T(8,128)(2,1)}, bf16[64,5120]{1,0:T(8,128)(2,1)}, u32[]{:S(2)}, u32[]{:S(2)}) collective-permute-start(bf16[64,5120]{1,0:T(8,128)(2,1)} %collective-permute-done.24.refs_3_), channel_id=1, source_target_pairs={{0,12},{4,8},{8,4},{12,0},{16,28},{20,24},{24,20},{28,16},{32,44},... | collective-permute-start | bytes 1966088 | tf_op jit(solution)/shard_map/ppermute | solution.py:44
  203.6 30.4 %collective-permute-start.29 = (bf16[1280,320]{0,1:T(8,128)(2,1)}, bf16[1280,320]{0,1:T(8,128)(2,1)S(1)}, u32[]{:S(2)}, u32[]{:S(2)}) collective-permute-start(bf16[1280,320]{0,1:T(8,128)(2,1)} %copy.52), channel_id=1, source_target_pairs={{0,64},{1,65},{2,66},{3,67},{4,68},{5,69},{6,70},{7,71},{8,72},{9,... | collective-permute-start | bytes 2457608 | tf_op jit(solution)/shard_map/ppermute | solution.py:33
  225.1 15.8 %all-to-all-start.2 = ((bf16[8,64,640]{2,1,0:T(8,128)(2,1)}), bf16[8,64,640]{2,1,0:T(8,128)(2,1)}, u32[]{:S(2)}, u32[]{:S(2)}) async-start(bf16[8,64,640]{2,1,0:T(8,128)(2,1)} %product.7), calls=%async_computation.2 | async-start | bytes 1310720 | tf_op jit(solution)/shard_map/all_to_all | solution.py:131
  242.9 1.1 copy-start.6
